TPU v7x, 32 devices: a whole 2x2x4 slice. The times are simulated.
32 devices in a mesh: freq: 2 (over y), harm: 4 (over z), wall: 4 (over x, core).
Axes of the slice: x: 2, y: 2, z: 4, core: 2. Of those that a mesh axis runs over, the one named last changes fastest.
Arguments:
- sketch: bfloat16 [32, 1024, 128], P(('freq', 'harm'), 'wall'), parts along dimension 0, may hold values from -48 to 48
- inverse_blocks: bfloat16 [32, 1024, 1024], P(('freq', 'harm'), 'wall'), parts along dimension 0, may hold values from -0.1875 to 0.1875
- couple_up: bfloat16 [8, 1024, 1024], P('freq', 'wall'), parts along dimension 0, may hold values from -0.03125 to 0.03125
- couple_down: bfloat16 [8, 1024, 1024], P('freq', 'wall'), parts along dimension 0, may hold values from -0.03125 to 0.03125
- strip_harmonics: int32 [8], P('freq'), parts along dimension 0, may hold values from 0 to 3
Outputs:
- basis: float32 [32, 1024, 128], P(('freq', 'harm'), 'wall'), parts along dimension 0
- triangle: float32 [256, 128], P('freq'), parts along dimension 0
There are 2 independent parts, one for each index of `freq`. A program takes and returns all parts, laid end to end along the dimension named above; each array names one. Nothing has to cross between parts.
Inputs may be any that keep to these rules, and one draw needn't show every extreme that they name: `strip_harmonics`: each entry one of 0 to 3; entries may repeat.
All inputs are finite; a program needn't handle non-finite values.
Results may differ from a plain program's by a relative error of at most 0.0045.
Values may be sent and summed in bfloat16 or wider, within the bound.
No kernel may reach another device: no remote copies, remote signals or barrier semaphores. Data moves between devices by JAX's collectives and lax.ppermute only.
A program may use at most 64 MiB of HBM per device.

v0:
```python
import jax
import jax.numpy as jnp
from jax import lax
from jax.sharding import PartitionSpec as P

BAND = 4
SWEEPS = 3


def padded(cells, sides, width):
    for axis, dim in sides:
        count = lax.axis_size(axis)
        head = lax.slice_in_dim(cells, 0, width, axis=dim)
        tail = lax.slice_in_dim(cells, cells.shape[dim] - width, cells.shape[dim], axis=dim)
        cells = jnp.concatenate(
            [
                lax.ppermute(tail, axis, [(i, (i + 1) % count) for i in range(count)]),
                cells,
                lax.ppermute(head, axis, [((i + 1) % count, i) for i in range(count)]),
            ],
            axis=dim,
        )
    return cells


def body(sketch, inverse_blocks, couple_up, couple_down, strip_harmonics):
    offsets = strip_harmonics + 1
    local_count = sketch.shape[0]
    row_count = sketch.shape[1]
    width = sketch.shape[2]
    empty = jnp.zeros((local_count, row_count, width), jnp.float32)

    def add_inverse(piece):
        return jnp.einsum("hrc,hck->hrk", inverse_blocks, piece, preferred_element_type=jnp.float32)

    def apply_inverse(source):
        return add_inverse(lax.all_gather(source, "wall", axis=1, tiled=True))

    state = apply_inverse(sketch).astype(jnp.bfloat16)
    sampled = None
    for sweep in range(SWEEPS):
        extended = padded(state, (("harm", 0),), BAND)
        total = empty
        add_piece = lax.all_gather(extended, "wall", axis=1, tiled=True)
        for j in range(BAND):
            up_cols = couple_up[j]
            down_cols = couple_down[j]
            below = lax.dynamic_slice_in_dim(add_piece, BAND - offsets[j], local_count, 0)
            above = lax.dynamic_slice_in_dim(add_piece, BAND + offsets[j], local_count, 0)
            total = total + jnp.einsum(
                "rc,hck->hrk", up_cols, below, preferred_element_type=jnp.float32
            )
            total = total + jnp.einsum(
                "rc,hck->hrk", down_cols, above, preferred_element_type=jnp.float32
            )
        rhs = (sketch.astype(jnp.float32) - total).astype(jnp.bfloat16)
        result = apply_inverse(rhs)
        if sweep < SWEEPS - 1:
            state = result.astype(jnp.bfloat16)
        else:
            sampled = result
    flat = sampled.reshape(local_count * row_count, width)
    count = lax.axis_size("harm") * lax.axis_size("wall") * local_count * row_count
    local_gram = jnp.dot(
        flat.T, flat, precision=lax.Precision.HIGHEST, preferred_element_type=jnp.float32
    )
    gram = lax.psum(local_gram, ("harm", "wall")) / count
    lower = jnp.linalg.cholesky(gram)
    basis = jax.scipy.linalg.solve_triangular(lower, flat.T, lower=True).T
    triangle = lower.T
    return (basis.reshape(local_count, row_count, width), triangle)


def solution(mesh):
    return jax.shard_map(
        body,
        mesh=mesh,
        in_specs=(
            P(("freq", "harm"), "wall", None),
            P(("freq", "harm"), "wall", None),
            P("freq", "wall", None),
            P("freq", "wall", None),
            P("freq"),
        ),
        out_specs=(P(("freq", "harm"), "wall", None), P("freq", None)),
        check_vma=False,
    )
```

profile of v0, /device:TPU:0, one launch (start us, length us, event | category | flops | bytes accessed | tf_op | source)
XLA Modules:
  0.0 369.7 jit_solution(4480394632407928866)
XLA Ops:
  7.2 0.7 all-gather.8.cloned.1.call-update
  8.0 21.0 %all-gather.8.cloned.1.call-done = bf16[4,1024,128]{2,1,0:T(8,128)(2,1)} async-done(((bf16[4,256,128]{2,1,0:T(8,128)(2,1)}), bf16[4,1024,128]{2,1,0:T(8,128)(2,1)}) %all-gather.8.cloned.1.call-update) | async-done | bytes 1048592 | tf_op jit(solution)/shard_map/all_gather | solution.py:37
  29.0 1.9 convolution_convert_fusion.2
  31.0 3.4 collective-permute-start.1
  34.3 6.7 %collective-permute-done.1 = bf16[4,256,128]{2,1,0:T(8,128)(2,1)S(1)} collective-permute-done((bf16[4,256,128]{2,1,0:T(8,128)(2,1)S(1)}, bf16[4,256,128]{2,1,0:T(8,128)(2,1)S(1)}, u32[]{:S(2)}, u32[]{:S(2)}) %collective-permute-start.1) | collective-permute-done | bytes 262176 | tf_op jit(solution)/shard_map/ppermute | solution.py:19
  41.1 5.8 %collective-permute-done = bf16[4,256,128]{2,1,0:T(8,128)(2,1)S(1)} collective-permute-done((bf16[4,256,128]{2,1,0:T(8,128)(2,1)S(1)}, bf16[4,256,128]{2,1,0:T(8,128)(2,1)S(1)}, u32[]{:S(2)}, u32[]{:S(2)}) %collective-permute-start) | collective-permute-done | bytes 262176 | tf_op jit(solution)/shard_map/ppermute | solution.py:17
  46.9 1.0 pad_maximum_fusion
  48.0 0.7 fusion.114
  58.8 16.2 %all-gather.10.cloned.1.call-done = bf16[12,1024,128]{2,1,0:T(8,128)(2,1)} async-done(((bf16[12,256,128]{2,1,0:T(8,128)(2,1)}), bf16[12,1024,128]{2,1,0:T(8,128)(2,1)}) %all-gather.10.cloned.1.call-update) | async-done | bytes 3145744 | tf_op jit(solution)/shard_map/all_gather | solution.py:44
  75.0 2.0 fusion.35
  77.0 1.9 convolution_add_fusion.20
  78.9 1.7 convolution_add_fusion.19
  81.1 0.5 convolution_add_fusion.17
  82.6 1.2 fusion.8
  83.9 16.9 %all-gather.12.cloned.1.call-done = bf16[4,1024,128]{1,2,0:T(8,128)(2,1)} async-done(((bf16[4,256,128]{1,2,0:T(8,128)(2,1)}), bf16[4,1024,128]{1,2,0:T(8,128)(2,1)}) %all-gather.12.cloned.1.call-update) | async-done | bytes 1048592 | tf_op jit(solution)/shard_map/all_gather | solution.py:37
  100.8 2.1 fusion.9
  102.9 3.4 collective-permute-start.3
  106.3 6.7 %collective-permute-done.3 = bf16[4,256,128]{1,2,0:T(8,128)(2,1)S(1)} collective-permute-done((bf16[4,256,128]{1,2,0:T(8,128)(2,1)S(1)}, bf16[4,256,128]{1,2,0:T(8,128)(2,1)S(1)}, u32[]{:S(2)}, u32[]{:S(2)}) %collective-permute-start.3) | collective-permute-done | bytes 262176 | tf_op jit(solution)/shard_map/ppermute | solution.py:19
  113.0 5.8 %collective-permute-done.2 = bf16[4,256,128]{1,2,0:T(8,128)(2,1)S(1)} collective-permute-done((bf16[4,256,128]{1,2,0:T(8,128)(2,1)S(1)}, bf16[4,256,128]{1,2,0:T(8,128)(2,1)S(1)}, u32[]{:S(2)}, u32[]{:S(2)}) %collective-permute-start.2) | collective-permute-done | bytes 262176 | tf_op jit(solution)/shard_map/ppermute | solution.py:17
  118.9 1.0 pad_maximum_fusion.1
  119.9 27.4 %all-gather.14.cloned.1.call-done = bf16[12,1024,128]{1,2,0:T(8,128)(2,1)} async-done(((bf16[12,256,128]{1,2,0:T(8,128)(2,1)}), bf16[12,1024,128]{1,2,0:T(8,128)(2,1)}) %all-gather.14.cloned.1.call-update) | async-done | bytes 3145744 | tf_op jit(solution)/shard_map/all_gather | solution.py:44
  147.3 2.0 fusion.26
  149.4 1.8 convolution_add_fusion.13
  151.3 1.7 convolution_add_fusion.12
  154.9 1.2 fusion.7
  156.2 16.9 %all-gather.16.cloned.1.call-done = bf16[4,1024,128]{1,2,0:T(8,128)(2,1)} async-done(((bf16[4,256,128]{1,2,0:T(8,128)(2,1)}), bf16[4,1024,128]{1,2,0:T(8,128)(2,1)}) %all-gather.16.cloned.1.call-update) | async-done | bytes 1048592 | tf_op jit(solution)/shard_map/all_gather | solution.py:37
  173.1 2.1 fusion.10
  175.2 3.4 collective-permute-start.5
  178.6 6.7 %collective-permute-done.5 = bf16[4,256,128]{1,2,0:T(8,128)(2,1)S(1)} collective-permute-done((bf16[4,256,128]{1,2,0:T(8,128)(2,1)S(1)}, bf16[4,256,128]{1,2,0:T(8,128)(2,1)S(1)}, u32[]{:S(2)}, u32[]{:S(2)}) %collective-permute-start.5) | collective-permute-done | bytes 262176 | tf_op jit(solution)/shard_map/ppermute | solution.py:19
  185.3 5.8 %collective-permute-done.4 = bf16[4,256,128]{1,2,0:T(8,128)(2,1)S(1)} collective-permute-done((bf16[4,256,128]{1,2,0:T(8,128)(2,1)S(1)}, bf16[4,256,128]{1,2,0:T(8,128)(2,1)S(1)}, u32[]{:S(2)}, u32[]{:S(2)}) %collective-permute-start.4) | collective-permute-done | bytes 262176 | tf_op jit(solution)/shard_map/ppermute | solution.py:17
  191.2 1.0 pad_maximum_fusion.2
  192.4 27.2 %all-gather.18.cloned.1.call-done = bf16[12,1024,128]{1,2,0:T(8,128)(2,1)} async-done(((bf16[12,256,128]{1,2,0:T(8,128)(2,1)}), bf16[12,1024,128]{1,2,0:T(8,128)(2,1)}) %all-gather.18.cloned.1.call-update) | async-done | bytes 3145744 | tf_op jit(solution)/shard_map/all_gather | solution.py:44
  219.6 2.0 fusion.17
  221.7 1.8 convolution_add_fusion.6
  223.6 1.7 convolution_add_fusion.5
  227.2 1.2 fusion.6
  228.5 16.9 %all-gather.20.cloned.1.call-done = bf16[4,1024,128]{1,2,0:T(8,128)(2,1)} async-done(((bf16[4,256,128]{1,2,0:T(8,128)(2,1)}), bf16[4,1024,128]{1,2,0:T(8,128)(2,1)}) %all-gather.20.cloned.1.call-update) | async-done | bytes 1048592 | tf_op jit(solution)/shard_map/all_gather | solution.py:37
  245.4 2.1 convolution_bitcast_fusion
  247.5 1.2 convolution_bitcast_fusion.1
  248.7 87.0 %all-reduce.2.cloned.1.call-done = f32[128,128]{0,1:T(8,128)} async-done(((f32[128,128]{0,1:T(8,128)}), f32[128,128]{0,1:T(8,128)}) %all-reduce.2.cloned.1.call-update) | async-done | bytes 65552 | tf_op jit(solution)/shard_map/psum | solution.py:67
  335.7 0.8 broadcast_multiply_fusion
  336.6 0.9 fusion.88
  337.5 11.7 %cholesky.16 = f32[128,128]{1,0:T(8,128)S(1)} custom-call(f32[128,128]{1,0:T(8,128)S(1)} %fusion.88), custom_call_target="Cholesky" | custom-call | tf_op jit(solution)/shard_map/jit(cholesky)/cholesky | solution.py:68
  349.2 0.6 compare_reduce_fusion
  349.9 0.7 fusion.89
  350.5 0.7 copy.13
  351.3 9.8 %custom-call.7 = f32[1,128,128]{1,2,0:T(8,128)S(1)} custom-call(f32[1,128,128]{2,1,0:T(8,128)S(1)} %get-tuple-element.5), custom_call_target="InvertDiagBlocksLowerTriangular" | custom-call | tf_op jit(solution)/shard_map/jit(_solve_triangular)/triangular_solve | solution.py:69
  361.1 1.8 fusion.86
  (57 shorter events, 6.4 us)
Async XLA Ops:
  7.2 21.8 %copy-start = (bf16[4,256,1024]{2,1,0:T(8,128)(2,1)S(1)}, bf16[4,256,1024]{2,1,0:T(8,128)(2,1)}, u32[]{:S(2)}) copy-start(bf16[4,256,1024]{2,1,0:T(8,128)(2,1)} %param.6) | copy-start | bytes 6291460
  7.2 21.8 %all-gather.8.cloned.1.call-start = ((), (), s32[]{:S(2)}) async-start(), calls=%async_computation | async-start | bytes 1310720 | tf_op jit(solution)/shard_map/all_gather | solution.py:37
  7.9 67.1 %all-gather.10.cloned.1.call-start = ((), (), s32[]{:S(2)}) async-start(), calls=%async_computation.1 | async-start | bytes 3932160 | tf_op jit(solution)/shard_map/all_gather | solution.py:44
  30.9 17.0 %copy-start.11 = (s32[4]{0:T(128)S(1)}, s32[4]{0:T(128)}, u32[]{:S(2)}) copy-start(s32[4]{0:T(128)} %param.9) | copy-start | bytes 52
  30.9 27.6 %copy-start.10 = (bf16[4,256,128]{2,1,0:T(8,128)(2,1)S(1)}, bf16[4,256,128]{2,1,0:T(8,128)(2,1)}, u32[]{:S(2)}) copy-start(bf16[4,256,128]{2,1,0:T(8,128)(2,1)} %param.5) | copy-start | bytes 786436
  31.0 10.1 %collective-permute-start.1 = (bf16[4,256,128]{2,1,0:T(8,128)(2,1)S(1)}, bf16[4,256,128]{2,1,0:T(8,128)(2,1)S(1)}, u32[]{:S(2)}, u32[]{:S(2)}) collective-permute-start(bf16[4,256,128]{2,1,0:T(8,128)(2,1)S(1)} %convolution_convert_fusion.2), channel_id=1, source_target_pairs={{4,0},{8,4},{12,8},{0,12},{5,1},{9,5},{13,9},{1,13},{6,2},{10,6},{... | collective-permute-start | bytes 786440 | tf_op jit(solution)/shard_map/ppermute | solution.py:19
  34.3 12.6 %collective-permute-start = (bf16[4,256,128]{2,1,0:T(8,128)(2,1)S(1)}, bf16[4,256,128]{2,1,0:T(8,128)(2,1)S(1)}, u32[]{:S(2)}, u32[]{:S(2)}) collective-permute-start(bf16[4,256,128]{2,1,0:T(8,128)(2,1)S(1)} %convolution_convert_fusion.2), channel_id=1, source_target_pairs={{0,4},{4,8},{8,12},{12,0},{1,5},{5,9},{9,13},{13,1},{2,6},{6,10},{... | collective-permute-start | bytes 786440 | tf_op jit(solution)/shard_map/ppermute | solution.py:17
  47.9 52.9 %all-gather.12.cloned.1.call-start = ((), (), s32[]{:S(2)}) async-start(), calls=%async_computation.2 | async-start | bytes 1310720 | tf_op jit(solution)/shard_map/all_gather | solution.py:37
  75.0 2.1 copy-start.1
  77.0 3.6 copy-start.4
  77.0 3.6 copy-start.7
  83.9 63.5 %all-gather.14.cloned.1.call-start = ((), (), s32[]{:S(2)}) async-start(), calls=%async_computation.3 | async-start | bytes 3932160 | tf_op jit(solution)/shard_map/all_gather | solution.py:44
  102.9 10.1 %collective-permute-start.3 = (bf16[4,256,128]{1,2,0:T(8,128)(2,1)S(1)}, bf16[4,256,128]{1,2,0:T(8,128)(2,1)S(1)}, u32[]{:S(2)}, u32[]{:S(2)}) collective-permute-start(bf16[4,256,128]{1,2,0:T(8,128)(2,1)S(1)} %fusion.9), channel_id=1, source_target_pairs={{4,0},{8,4},{12,8},{0,12},{5,1},{9,5},{13,9},{1,13},{6,2},{10,6},{... | collective-permute-start | bytes 786440 | tf_op jit(solution)/shard_map/ppermute | solution.py:19
  106.3 12.6 %collective-permute-start.2 = (bf16[4,256,128]{1,2,0:T(8,128)(2,1)S(1)}, bf16[4,256,128]{1,2,0:T(8,128)(2,1)S(1)}, u32[]{:S(2)}, u32[]{:S(2)}) collective-permute-start(bf16[4,256,128]{1,2,0:T(8,128)(2,1)S(1)} %fusion.9), channel_id=1, source_target_pairs={{0,4},{4,8},{8,12},{12,0},{1,5},{5,9},{9,13},{13,1},{2,6},{6,10},{... | collective-permute-start | bytes 786440 | tf_op jit(solution)/shard_map/ppermute | solution.py:17
  119.9 53.3 %all-gather.16.cloned.1.call-start = ((), (), s32[]{:S(2)}) async-start(), calls=%async_computation.4 | async-start | bytes 1310720 | tf_op jit(solution)/shard_map/all_gather | solution.py:37
  147.3 2.1 copy-start.2
  149.4 3.6 copy-start.6
  149.4 3.6 copy-start.8
  156.2 63.5 %all-gather.18.cloned.1.call-start = ((), (), s32[]{:S(2)}) async-start(), calls=%async_computation.5 | async-start | bytes 3932160 | tf_op jit(solution)/shard_map/all_gather | solution.py:44
  175.2 10.1 %collective-permute-start.5 = (bf16[4,256,128]{1,2,0:T(8,128)(2,1)S(1)}, bf16[4,256,128]{1,2,0:T(8,128)(2,1)S(1)}, u32[]{:S(2)}, u32[]{:S(2)}) collective-permute-start(bf16[4,256,128]{1,2,0:T(8,128)(2,1)S(1)} %fusion.10), channel_id=1, source_target_pairs={{4,0},{8,4},{12,8},{0,12},{5,1},{9,5},{13,9},{1,13},{6,2},{10,6},{... | collective-permute-start | bytes 786440 | tf_op jit(solution)/shard_map/ppermute | solution.py:19
  178.6 12.6 %collective-permute-start.4 = (bf16[4,256,128]{1,2,0:T(8,128)(2,1)S(1)}, bf16[4,256,128]{1,2,0:T(8,128)(2,1)S(1)}, u32[]{:S(2)}, u32[]{:S(2)}) collective-permute-start(bf16[4,256,128]{1,2,0:T(8,128)(2,1)S(1)} %fusion.10), channel_id=1, source_target_pairs={{0,4},{4,8},{8,12},{12,0},{1,5},{5,9},{9,13},{13,1},{2,6},{6,10},{... | collective-permute-start | bytes 786440 | tf_op jit(solution)/shard_map/ppermute | solution.py:17
  192.2 53.3 %all-gather.20.cloned.1.call-start = ((), (), s32[]{:S(2)}) async-start(), calls=%async_computation.6 | async-start | bytes 1310720 | tf_op jit(solution)/shard_map/all_gather | solution.py:37
  219.6 2.1 copy-start.3
  221.7 3.6 copy-start.5
  221.7 3.6 copy-start.9
  228.5 107.2 %all-reduce.2.cloned.1.call-start = ((), (), s32[]{:S(2)}) async-start(), calls=%async_computation.7 | async-start | bytes 131072 | tf_op jit(solution)/shard_map/psum | solution.py:67
Sparse Core Ops, SparseCore 0:
  9.5 19.4 all-gather.7
  48.0 26.9 all-gather.9
  84.0 16.8 all-gather.11
  120.0 27.3 all-gather.13
  156.3 16.8 all-gather.15
  192.3 27.3 all-gather.17
  228.6 16.8 all-gather.19
  249.5 86.1 all-reduce.1
where the time goes:
time: 371 us; the launch traced here: 370 us
  waiting for transfers between devices  268 us (72%)
  matrix products  37.1 us (10%)
  other arithmetic  27.5 us (7%)
  between operations  24.5 us (7%)
  starting transfers between devices  10.7 us (3%)
    psum x1, waiting for transfers between devices, body(): gram = lax.psum(local_gram, ('harm', 'wall')) / count  87 us
    all_gather x4, waiting for transfers between devices, apply_inverse(): return add_inverse(lax.all_gather(source, 'wall', axis=1, tiled=True))  71.8 us
    all_gather x3, waiting for transfers between devices, body(): add_piece = lax.all_gather(extended, 'wall', axis=1, tiled=True)  70.8 us
    ppermute x3, waiting for transfers between devices, padded(): lax.ppermute(head, axis, [((i + 1) % count, i) for i in range(count)])  20.2 us
    ppermute x3, waiting for transfers between devices, padded(): lax.ppermute(tail, axis, [(i, (i + 1) % count) for i in range(count)])  17.5 us
    dot_general x12, matrix products, body(): jnp.einsum('rc,hck->hrk', up_cols, below, preferred_element_type=jnp.floa...  13.6 us
    dot_general x12, matrix products, body(): jnp.einsum('rc,hck->hrk', down_cols, above, preferred_element_type=jnp.fl...  12.4 us
    another operation x3, other arithmetic, body(): lower = jnp.linalg.cholesky(gram)  12.4 us
  transfers between devices with their start and end apart: 14, of which 14 were waited for; matrix products, arithmetic and copies ran while one was open for 0% of the time, Pallas kernels for 0%

commit v1 on v0

v1 whole, which is shorter than its diff:
```python
import functools

import jax
import jax.numpy as jnp
from jax import lax
from jax.experimental import pallas as pl
from jax.experimental.pallas import tpu as pltpu
from jax.sharding import PartitionSpec as P

BAND = 4
SWEEPS = 3
F32 = jnp.float32
BF16 = jnp.bfloat16
VMEM = pl.BlockSpec(memory_space=pltpu.VMEM)
SMEM = pl.BlockSpec(memory_space=pltpu.SMEM)


def flip(value, axis, mask):
    return lax.ppermute(value, axis, [(i, i ^ mask) for i in range(lax.axis_size(axis))])


def turn(value, axis, step):
    count = lax.axis_size(axis)
    return lax.ppermute(value, axis, [(i, (i + step) % count) for i in range(count)])


def wall_pieces(own):
    pieces = {0: own}
    bit = lax.axis_size("wall") // 2
    while bit:
        for mask in list(pieces):
            pieces[mask ^ bit] = flip(pieces[mask], "wall", bit)
        bit //= 2
    return [pieces[mask] for mask in range(len(pieces))]


def columns_of(place, mask, rows):
    return pl.ds(pl.multiple_of((place ^ mask) * rows, rows), rows)


def params(mib):
    return pltpu.CompilerParams(vmem_limit_bytes=mib << 20)


def inverse_kernel(shards, with_gram, place_ref, blocks_ref, *refs):
    pieces, outs = refs[:shards], refs[shards:]
    count, rows, width = pieces[0].shape
    place = place_ref[0]
    gram = jnp.zeros((width, width), F32)
    for h in range(count):
        total = jnp.zeros((rows, width), F32)
        for mask in range(shards):
            total += jnp.dot(
                blocks_ref[h, :, columns_of(place, mask, rows)],
                pieces[mask][h],
                preferred_element_type=F32,
            )
        outs[0][h] = total.astype(outs[0].dtype)
        if with_gram:
            gram += lax.dot_general(
                total,
                total,
                (((0,), (0,)), ((), ())),
                precision=lax.Precision.HIGHEST,
                preferred_element_type=F32,
            )
    if with_gram:
        outs[1][...] = gram


def apply_inverse(place, blocks, source, last):
    pieces = wall_pieces(source)
    shape, width = source.shape, source.shape[2]
    out = [jax.ShapeDtypeStruct(shape, F32 if last else BF16)]
    if last:
        out.append(jax.ShapeDtypeStruct((width, width), F32))
    return pl.pallas_call(
        functools.partial(inverse_kernel, len(pieces), last),
        out_shape=out,
        in_specs=[SMEM, VMEM] + [VMEM] * len(pieces),
        out_specs=[VMEM] * len(out),
        compiler_params=params(12),
    )(place, blocks, *pieces)


def couple_kernel(shards, place_ref, strip_ref, up_ref, down_ref, *refs):
    pieces = refs[:shards]
    own_ref, below_ref, above_ref, total = refs[shards:]
    count, rows, width = pieces[0].shape
    place = place_ref[0]
    total[...] = jnp.zeros_like(total)
    wide = [jnp.concatenate([p[h] for h in range(count)], axis=1) for p in pieces]
    for j in range(BAND):
        offset = strip_ref[j] + 1
        for weights, shift in ((up_ref, offset), (down_ref, -offset)):
            part = jnp.zeros((rows, count * width), F32)
            for mask in range(shards):
                part += jnp.dot(
                    weights[j, :, columns_of(place, mask, rows)],
                    wide[mask],
                    preferred_element_type=F32,
                )
            for h in range(count):
                total[BAND + shift + h] += part[:, h * width : (h + 1) * width]
    own_ref[...] = total[BAND : BAND + count]
    below_ref[...] = total[:BAND].astype(below_ref.dtype)
    above_ref[...] = total[BAND + count :].astype(above_ref.dtype)


def couple(place, strips, up, down, state):
    pieces = wall_pieces(state)
    count, rows, width = state.shape
    own, below, above = pl.pallas_call(
        functools.partial(couple_kernel, len(pieces)),
        out_shape=[
            jax.ShapeDtypeStruct((count, rows, width), F32),
            jax.ShapeDtypeStruct((BAND, rows, width), BF16),
            jax.ShapeDtypeStruct((BAND, rows, width), BF16),
        ],
        in_specs=[SMEM, SMEM, VMEM, VMEM] + [VMEM] * len(pieces),
        out_specs=[VMEM] * 3,
        scratch_shapes=[pltpu.VMEM((count + 2 * BAND, rows, width), F32)],
        compiler_params=params(20),
    )(place, strips, up, down, *pieces)
    from_before = turn(above, "harm", 1)
    from_after = turn(below, "harm", -1)
    return own, from_before, from_after


def all_sum(value):
    for axis in ("wall", "harm"):
        bit = 1
        while bit < lax.axis_size(axis):
            value = value + flip(value, axis, bit)
            bit *= 2
    return value


def body(sketch, inverse_blocks, couple_up, couple_down, strip_harmonics):
    count, rows, width = sketch.shape
    place = lax.axis_index("wall").astype(jnp.int32).reshape(1)
    (state,) = apply_inverse(place, inverse_blocks, sketch, False)
    for sweep in range(SWEEPS):
        own, before, after = couple(place, strip_harmonics, couple_up, couple_down, state)
        coupled = own
        if count == BAND:
            coupled = own + before.astype(F32) + after.astype(F32)
        else:
            coupled = coupled.at[:BAND].add(before.astype(F32))
            coupled = coupled.at[count - BAND :].add(after.astype(F32))
        rhs = (sketch.astype(F32) - coupled).astype(BF16)
        if sweep < SWEEPS - 1:
            (state,) = apply_inverse(place, inverse_blocks, rhs, False)
        else:
            sampled, gram = apply_inverse(place, inverse_blocks, rhs, True)
    entries = lax.axis_size("harm") * lax.axis_size("wall") * count * rows
    gram = all_sum(gram) / entries
    lower = jnp.linalg.cholesky(gram)
    flat = sampled.reshape(count * rows, width)
    basis = jax.scipy.linalg.solve_triangular(lower, flat.T, lower=True).T
    return (basis.reshape(count, rows, width), lower.T)


def solution(mesh):
    return jax.shard_map(
        body,
        mesh=mesh,
        in_specs=(
            P(("freq", "harm"), "wall", None),
            P(("freq", "harm"), "wall", None),
            P("freq", "wall", None),
            P("freq", "wall", None),
            P("freq"),
        ),
        out_specs=(P(("freq", "harm"), "wall", None), P("freq", None)),
        check_vma=False,
    )
```

time: 371 us -> 174 us (0.47)
  waiting for transfers between devices: 268 us -> 101 us
  matrix products: 37.1 us -> 1.36 us
  between operations: 24.5 us -> 0.79 us
  starting transfers between devices: 10.7 us -> 28.8 us
  Pallas kernels: 0 us -> 13.2 us
  other arithmetic: 27.5 us -> 23.3 us
    all_gather x7 -> x0, waiting for transfers between devices: 143 us -> none  [the longest x4 71.8 us: apply_inverse(): return add_inverse(lax.all_gather(source, 'wall', axis=1, tiled=True))]
    psum x1 -> x0, waiting for transfers between devices: 87 us -> none  [body(): gram = lax.psum(local_gram, ('harm', 'wall')) / count]
    ppermute x6 -> x31, waiting for transfers between devices: 37.7 us -> 101 us  [the longest x25 67.4 us: flip(): lax.ppermute(value, axis, [(i, i ^ mask) for i in range(lax.axis_size(axi...]
    dot_general x29 -> x0, matrix products: 35.3 us -> none  [the longest x12 13.6 us: body(): jnp.einsum('rc,hck->hrk', up_cols, below, preferred_element_type=jnp.floa...]
    ppermute x6 -> x31, starting transfers between devices: 10.2 us -> 28.8 us  [the longest x25 17.1 us: flip(): lax.ppermute(value, axis, [(i, i ^ mask) for i in range(lax.axis_size(axi...]
    pallas_call x0 -> x7, Pallas kernels: none -> 13.2 us  [the longest x3 9.4 us: couple(): pl.pallas_call(functools.partial(couple_kernel, len(pieces)), out_shape=[...]
    unnamed x26 -> x15, local copies, waits for them, and re-layouts: 1.14 us -> 4.88 us
  transfers between devices with their start and end apart: 14 -> 31, of which waited for: 14 -> 24; matrix products, arithmetic and copies ran while one was open for 0% -> 0% of each run, Pallas kernels for 0% -> 0%
where the time goes in v1:
time: 174 us; the launch traced here: 173 us
  waiting for transfers between devices  101 us (58%)
  starting transfers between devices  28.8 us (17%)
  other arithmetic  23.3 us (13%)
  Pallas kernels  13.2 us (8%)
  local copies, waits for them, and re-layouts  5.05 us (3%)
    ppermute x25, waiting for transfers between devices, flip(): lax.ppermute(value, axis, [(i, i ^ mask) for i in range(lax.axis_size(axi...  67.4 us
    ppermute x6, waiting for transfers between devices, turn(): lax.ppermute(value, axis, [(i, (i + step) % count) for i in range(count)])  33.6 us
    ppermute x25, starting transfers between devices, flip(): lax.ppermute(value, axis, [(i, i ^ mask) for i in range(lax.axis_size(axi...  17.1 us
    another operation x3, other arithmetic, body(): lower = jnp.linalg.cholesky(gram)  12.4 us
    ppermute x6, starting transfers between devices, turn(): lax.ppermute(value, axis, [(i, (i + step) % count) for i in range(count)])  11.7 us
    another operation x1, other arithmetic, body(): basis = jax.scipy.linalg.solve_triangular(lower, flat.T, lower=True).T  9.81 us
    pallas_call x3, Pallas kernels, couple(): pl.pallas_call(functools.partial(couple_kernel, len(pieces)), out_shape=[...  9.4 us
    unnamed x15, local copies, waits for them, and re-layouts  4.88 us
  transfers between devices with their start and end apart: 31, of which 24 were waited for; matrix products, arithmetic and copies ran while one was open for 0% of the time, Pallas kernels for 0%

profile of v1, /device:TPU:0, one launch (start us, length us, event | category | flops | bytes accessed | tf_op | source)
XLA Modules:
  0.0 173.4 jit_solution(3647912589800181356)
XLA Ops:
  0.6 3.0 %collective-permute-start.1 = (bf16[4,256,128]{2,1,0:T(8,128)(2,1)}, bf16[4,256,128]{2,1,0:T(8,128)(2,1)S(1)}, u32[]{:S(2)}, u32[]{:S(2)}) collective-permute-start(bf16[4,256,128]{2,1,0:T(8,128)(2,1)} %refs_0_.1), channel_id=1, source_target_pairs={{0,2},{1,3},{2,0},{3,1},{4,6},{5,7},{6,4},{7,5},{8,10},{9,11},{10,... | collective-permute-start | bytes 786440 | tf_op jit(solution)/shard_map/ppermute | solution.py:19
  3.7 6.5 %collective-permute-done.1.refs_2_ = bf16[4,256,128]{2,1,0:T(8,128)(2,1)S(1)} collective-permute-done((bf16[4,256,128]{2,1,0:T(8,128)(2,1)}, bf16[4,256,128]{2,1,0:T(8,128)(2,1)S(1)}, u32[]{:S(2)}, u32[]{:S(2)}) %collective-permute-start.1) | collective-permute-done | bytes 262176 | tf_op jit(solution)/shard_map/ppermute | solution.py:19
  10.2 1.5 collective-permute-done.2.refs_3_
  11.7 1.6 copy-done
  13.3 0.9 copy-done.4
  15.0 1.8 %collective-permute-start.4 = (bf16[4,256,128]{2,1,0:T(8,128)(2,1)S(1)}, bf16[4,256,128]{2,1,0:T(8,128)(2,1)S(1)}, u32[]{:S(2)}, u32[]{:S(2)}) collective-permute-start(bf16[4,256,128]{2,1,0:T(8,128)(2,1)S(1)} %shard_map.68.refs_0_), channel_id=1, source_target_pairs={{0,2},{1,3},{2,0},{3,1},{4,6},{5,7},{6,4},{7,5},{8,10},{9,11},{10,... | collective-permute-start | bytes 786440 | tf_op jit(solution)/shard_map/ppermute | solution.py:19
  16.8 6.6 %collective-permute-done.4.refs_2_ = bf16[4,256,128]{2,1,0:T(8,128)(2,1)S(1)} collective-permute-done((bf16[4,256,128]{2,1,0:T(8,128)(2,1)S(1)}, bf16[4,256,128]{2,1,0:T(8,128)(2,1)S(1)}, u32[]{:S(2)}, u32[]{:S(2)}) %collective-permute-start.4) | collective-permute-done | bytes 262176 | tf_op jit(solution)/shard_map/ppermute | solution.py:19
  23.4 1.5 collective-permute-done.5.refs_3_
  24.9 1.6 copy-done.3
  26.5 3.1 %shard_map.69 = (f32[4,256,128]{2,1,0:T(8,128)S(1)}, bf16[4,256,128]{2,1,0:T(8,128)(2,1)S(1)}, bf16[4,256,128]{2,1,0:T(8,128)(2,1)S(1)}) custom-call(s32[1]{0:T(128)} %bitcast.place_ref, s32[4]{0:T(128)S(1)} %copy-done.6, bf16[4,256,1024]{2,1,0:T(8,128)(2,1)S(1)} %copy-done.2, bf16[4,256,1024]{2,1,0:T(8,128)(2,1)S(1)} %copy-done.3, ...), custom_call_target="tpu_custom_call" | custom-call | tf_op jit(solution)/shard_map/pallas_call | solution.py:113
  29.7 1.9 %collective-permute-start.6 = (bf16[4,256,128]{2,1,0:T(8,128)(2,1)S(1)}, bf16[4,256,128]{2,1,0:T(8,128)(2,1)S(1)}, u32[]{:S(2)}, u32[]{:S(2)}) collective-permute-start(bf16[4,256,128]{2,1,0:T(8,128)(2,1)S(1)} %get-tuple-element.14), channel_id=1, source_target_pairs={{0,4},{4,8},{8,12},{12,0},{1,5},{5,9},{9,13},{13,1},{2,6},{6,10},{... | collective-permute-start | bytes 786440 | tf_op jit(solution)/shard_map/ppermute | solution.py:24
  31.6 2.1 %collective-permute-start.7 = (bf16[4,256,128]{2,1,0:T(8,128)(2,1)S(1)}, bf16[4,256,128]{2,1,0:T(8,128)(2,1)S(1)}, u32[]{:S(2)}, u32[]{:S(2)}) collective-permute-start(bf16[4,256,128]{2,1,0:T(8,128)(2,1)S(1)} %get-tuple-element.15), channel_id=1, source_target_pairs={{0,12},{4,0},{8,4},{12,8},{1,13},{5,1},{9,5},{13,9},{2,14},{6,2},{... | collective-permute-start | bytes 786440 | tf_op jit(solution)/shard_map/ppermute | solution.py:24
  33.7 7.1 %collective-permute-done.6 = bf16[4,256,128]{2,1,0:T(8,128)(2,1)S(1)} collective-permute-done((bf16[4,256,128]{2,1,0:T(8,128)(2,1)S(1)}, bf16[4,256,128]{2,1,0:T(8,128)(2,1)S(1)}, u32[]{:S(2)}, u32[]{:S(2)}) %collective-permute-start.6) | collective-permute-done | bytes 262176 | tf_op jit(solution)/shard_map/ppermute | solution.py:24
  40.8 4.5 %collective-permute-done.7 = bf16[4,256,128]{2,1,0:T(8,128)(2,1)S(1)} collective-permute-done((bf16[4,256,128]{2,1,0:T(8,128)(2,1)S(1)}, bf16[4,256,128]{2,1,0:T(8,128)(2,1)S(1)}, u32[]{:S(2)}, u32[]{:S(2)}) %collective-permute-start.7) | collective-permute-done | bytes 262176 | tf_op jit(solution)/shard_map/ppermute | solution.py:24
  45.4 1.5 collective-permute-start.9
  46.9 6.2 %collective-permute-done.9.refs_2_ = bf16[4,256,128]{2,1,0:T(8,128)(2,1)S(1)} collective-permute-done((bf16[4,256,128]{2,1,0:T(8,128)(2,1)S(1)}, bf16[4,256,128]{2,1,0:T(8,128)(2,1)S(1)}, u32[]{:S(2)}, u32[]{:S(2)}) %collective-permute-start.9) | collective-permute-done | bytes 262176 | tf_op jit(solution)/shard_map/ppermute | solution.py:19
  53.1 1.5 collective-permute-done.10.refs_3_
  55.4 1.5 collective-permute-start.12
  56.9 6.9 %collective-permute-done.12.refs_2_ = bf16[4,256,128]{2,1,0:T(8,128)(2,1)S(1)} collective-permute-done((bf16[4,256,128]{2,1,0:T(8,128)(2,1)S(1)}, bf16[4,256,128]{2,1,0:T(8,128)(2,1)S(1)}, u32[]{:S(2)}, u32[]{:S(2)}) %collective-permute-start.12) | collective-permute-done | bytes 262176 | tf_op jit(solution)/shard_map/ppermute | solution.py:19
  63.8 1.5 collective-permute-done.13.refs_3_
  65.3 3.1 %shard_map.71 = (f32[4,256,128]{2,1,0:T(8,128)S(1)}, bf16[4,256,128]{2,1,0:T(8,128)(2,1)S(1)}, bf16[4,256,128]{2,1,0:T(8,128)(2,1)S(1)}) custom-call(s32[1]{0:T(128)} %bitcast.place_ref, s32[4]{0:T(128)S(1)} %copy-done.6, bf16[4,256,1024]{2,1,0:T(8,128)(2,1)S(1)} %copy-done.2, bf16[4,256,1024]{2,1,0:T(8,128)(2,1)S(1)} %copy-done.3, ...), custom_call_target="tpu_custom_call" | custom-call | tf_op jit(solution)/shard_map/pallas_call | solution.py:113
  68.4 1.7 %collective-permute-start.14 = (bf16[4,256,128]{2,1,0:T(8,128)(2,1)S(1)}, bf16[4,256,128]{2,1,0:T(8,128)(2,1)S(1)}, u32[]{:S(2)}, u32[]{:S(2)}) collective-permute-start(bf16[4,256,128]{2,1,0:T(8,128)(2,1)S(1)} %get-tuple-element.17), channel_id=1, source_target_pairs={{0,4},{4,8},{8,12},{12,0},{1,5},{5,9},{9,13},{13,1},{2,6},{6,10},{... | collective-permute-start | bytes 786440 | tf_op jit(solution)/shard_map/ppermute | solution.py:24
  70.2 2.1 %collective-permute-start.15 = (bf16[4,256,128]{2,1,0:T(8,128)(2,1)S(1)}, bf16[4,256,128]{2,1,0:T(8,128)(2,1)S(1)}, u32[]{:S(2)}, u32[]{:S(2)}) collective-permute-start(bf16[4,256,128]{2,1,0:T(8,128)(2,1)S(1)} %get-tuple-element.18), channel_id=1, source_target_pairs={{0,12},{4,0},{8,4},{12,8},{1,13},{5,1},{9,5},{13,9},{2,14},{6,2},{... | collective-permute-start | bytes 786440 | tf_op jit(solution)/shard_map/ppermute | solution.py:24
  72.3 7.2 %collective-permute-done.14 = bf16[4,256,128]{2,1,0:T(8,128)(2,1)S(1)} collective-permute-done((bf16[4,256,128]{2,1,0:T(8,128)(2,1)S(1)}, bf16[4,256,128]{2,1,0:T(8,128)(2,1)S(1)}, u32[]{:S(2)}, u32[]{:S(2)}) %collective-permute-start.14) | collective-permute-done | bytes 262176 | tf_op jit(solution)/shard_map/ppermute | solution.py:24
  79.5 4.4 %collective-permute-done.15 = bf16[4,256,128]{2,1,0:T(8,128)(2,1)S(1)} collective-permute-done((bf16[4,256,128]{2,1,0:T(8,128)(2,1)S(1)}, bf16[4,256,128]{2,1,0:T(8,128)(2,1)S(1)}, u32[]{:S(2)}, u32[]{:S(2)}) %collective-permute-start.15) | collective-permute-done | bytes 262176 | tf_op jit(solution)/shard_map/ppermute | solution.py:24
  84.0 1.5 collective-permute-start.17
  85.5 6.4 %collective-permute-done.17.refs_2_ = bf16[4,256,128]{2,1,0:T(8,128)(2,1)S(1)} collective-permute-done((bf16[4,256,128]{2,1,0:T(8,128)(2,1)S(1)}, bf16[4,256,128]{2,1,0:T(8,128)(2,1)S(1)}, u32[]{:S(2)}, u32[]{:S(2)}) %collective-permute-start.17) | collective-permute-done | bytes 262176 | tf_op jit(solution)/shard_map/ppermute | solution.py:19
  91.9 1.5 collective-permute-done.18.refs_3_
  94.2 1.5 collective-permute-start.20
  95.7 6.9 %collective-permute-done.20.refs_2_ = bf16[4,256,128]{2,1,0:T(8,128)(2,1)S(1)} collective-permute-done((bf16[4,256,128]{2,1,0:T(8,128)(2,1)S(1)}, bf16[4,256,128]{2,1,0:T(8,128)(2,1)S(1)}, u32[]{:S(2)}, u32[]{:S(2)}) %collective-permute-start.20) | collective-permute-done | bytes 262176 | tf_op jit(solution)/shard_map/ppermute | solution.py:19
  102.6 1.5 collective-permute-done.21.refs_3_
  104.1 3.1 %shard_map.73 = (f32[4,256,128]{2,1,0:T(8,128)S(1)}, bf16[4,256,128]{2,1,0:T(8,128)(2,1)S(1)}, bf16[4,256,128]{2,1,0:T(8,128)(2,1)S(1)}) custom-call(s32[1]{0:T(128)} %bitcast.place_ref, s32[4]{0:T(128)S(1)} %copy-done.6, bf16[4,256,1024]{2,1,0:T(8,128)(2,1)S(1)} %copy-done.2, bf16[4,256,1024]{2,1,0:T(8,128)(2,1)S(1)} %copy-done.3, ...), custom_call_target="tpu_custom_call" | custom-call | tf_op jit(solution)/shard_map/pallas_call | solution.py:113
  107.4 3.7 %collective-permute-start.23 = (bf16[4,256,128]{2,1,0:T(8,128)(2,1)S(1)}, bf16[4,256,128]{2,1,0:T(8,128)(2,1)S(1)}, u32[]{:S(2)}, u32[]{:S(2)}) collective-permute-start(bf16[4,256,128]{2,1,0:T(8,128)(2,1)S(1)} %get-tuple-element.21), channel_id=1, source_target_pairs={{0,12},{4,0},{8,4},{12,8},{1,13},{5,1},{9,5},{13,9},{2,14},{6,2},{... | collective-permute-start | bytes 786440 | tf_op jit(solution)/shard_map/ppermute | solution.py:24
  111.1 7.2 %collective-permute-done.22 = bf16[4,256,128]{2,1,0:T(8,128)(2,1)S(1)} collective-permute-done((bf16[4,256,128]{2,1,0:T(8,128)(2,1)S(1)}, bf16[4,256,128]{2,1,0:T(8,128)(2,1)S(1)}, u32[]{:S(2)}, u32[]{:S(2)}) %collective-permute-start.22) | collective-permute-done | bytes 262176 | tf_op jit(solution)/shard_map/ppermute | solution.py:24
  118.3 3.2 %collective-permute-done.23 = bf16[4,256,128]{2,1,0:T(8,128)(2,1)S(1)} collective-permute-done((bf16[4,256,128]{2,1,0:T(8,128)(2,1)S(1)}, bf16[4,256,128]{2,1,0:T(8,128)(2,1)S(1)}, u32[]{:S(2)}, u32[]{:S(2)}) %collective-permute-start.23) | collective-permute-done | bytes 262176 | tf_op jit(solution)/shard_map/ppermute | solution.py:24
  121.7 1.5 collective-permute-start.25
  123.1 6.1 %collective-permute-done.25.refs_2_ = bf16[4,256,128]{2,1,0:T(8,128)(2,1)S(1)} collective-permute-done((bf16[4,256,128]{2,1,0:T(8,128)(2,1)S(1)}, bf16[4,256,128]{2,1,0:T(8,128)(2,1)S(1)}, u32[]{:S(2)}, u32[]{:S(2)}) %collective-permute-start.25) | collective-permute-done | bytes 262176 | tf_op jit(solution)/shard_map/ppermute | solution.py:19
  129.2 1.5 collective-permute-done.26.refs_3_
  130.8 1.6 shard_map.74
  132.7 1.1 collective-permute-done.27
  133.9 1.5 collective-permute-start.28
  135.3 2.9 %collective-permute-done.28 = f32[128,128]{0,1:T(8,128)S(1)} collective-permute-done((f32[128,128]{0,1:T(8,128)S(1)}, f32[128,128]{0,1:T(8,128)S(1)}, u32[]{:S(2)}, u32[]{:S(2)}) %collective-permute-start.28) | collective-permute-done | bytes 65568 | tf_op jit(solution)/shard_map/ppermute | solution.py:19
  138.7 3.8 %collective-permute-done.29 = f32[128,128]{0,1:T(8,128)S(1)} collective-permute-done((f32[128,128]{0,1:T(8,128)S(1)}, f32[128,128]{0,1:T(8,128)S(1)}, u32[]{:S(2)}, u32[]{:S(2)}) %collective-permute-start.29) | collective-permute-done | bytes 65568 | tf_op jit(solution)/shard_map/ppermute | solution.py:19
  142.5 2.5 %collective-permute-start.30 = (f32[128,128]{0,1:T(8,128)S(1)}, f32[128,128]{0,1:T(8,128)S(1)}, u32[]{:S(2)}, u32[]{:S(2)}) collective-permute-start(f32[128,128]{0,1:T(8,128)S(1)} %add.50), channel_id=1, source_target_pairs={{0,8},{4,12},{8,0},{12,4},{1,9},{5,13},{9,1},{13,5},{2,10},{6,14},... | collective-permute-start | bytes 196616 | tf_op jit(solution)/shard_map/ppermute | solution.py:19
  145.1 3.3 %collective-permute-done.30 = f32[128,128]{0,1:T(8,128)S(1)} collective-permute-done((f32[128,128]{0,1:T(8,128)S(1)}, f32[128,128]{0,1:T(8,128)S(1)}, u32[]{:S(2)}, u32[]{:S(2)}) %collective-permute-start.30) | collective-permute-done | bytes 65568 | tf_op jit(solution)/shard_map/ppermute | solution.py:19
  148.5 11.7 %cholesky.16 = f32[128,128]{1,0:T(8,128)S(1)} custom-call(f32[128,128]{1,0:T(8,128)S(1)} %fusion.5), custom_call_target="Cholesky" | custom-call | tf_op jit(solution)/shard_map/jit(cholesky)/cholesky | solution.py:158
  162.3 9.8 %custom-call.7 = f32[1,128,128]{1,2,0:T(8,128)S(1)} custom-call(f32[1,128,128]{2,1,0:T(8,128)S(1)} %get-tuple-element.27), custom_call_target="InvertDiagBlocksLowerTriangular" | custom-call | tf_op jit(solution)/shard_map/jit(_solve_triangular)/triangular_solve | solution.py:160
  172.1 1.4 fusion.3
  (52 shorter events, 5.7 us)
Async XLA Ops:
  0.6 24.3 %copy-start.6 = (s32[4]{0:T(128)S(1)}, s32[4]{0:T(128)}, u32[]{:S(2)}) copy-start(s32[4]{0:T(128)} %strip_ref.5) | copy-start | bytes 52
  0.6 9.5 %collective-permute-start.1 = (bf16[4,256,128]{2,1,0:T(8,128)(2,1)}, bf16[4,256,128]{2,1,0:T(8,128)(2,1)S(1)}, u32[]{:S(2)}, u32[]{:S(2)}) collective-permute-start(bf16[4,256,128]{2,1,0:T(8,128)(2,1)} %refs_0_.1), channel_id=1, source_target_pairs={{0,2},{1,3},{2,0},{3,1},{4,6},{5,7},{6,4},{7,5},{8,10},{9,11},{10,... | collective-permute-start | bytes 786440 | tf_op jit(solution)/shard_map/ppermute | solution.py:19
  3.7 6.5 %collective-permute-start = (bf16[4,256,128]{2,1,0:T(8,128)(2,1)}, bf16[4,256,128]{2,1,0:T(8,128)(2,1)S(1)}, u32[]{:S(2)}, u32[]{:S(2)}) collective-permute-start(bf16[4,256,128]{2,1,0:T(8,128)(2,1)} %refs_0_.1), channel_id=1, source_target_pairs={{0,1},{1,0},{2,3},{3,2},{4,5},{5,4},{6,7},{7,6},{8,9},{9,8},{10,11... | collective-permute-start | bytes 786440 | tf_op jit(solution)/shard_map/ppermute | solution.py:19
  10.2 1.5 collective-permute-start.2
  11.7 1.6 copy-start
  13.3 0.9 copy-start.4
  14.3 10.7 %copy-start.2 = (bf16[4,256,1024]{2,1,0:T(8,128)(2,1)S(1)}, bf16[4,256,1024]{2,1,0:T(8,128)(2,1)}, u32[]{:S(2)}) copy-start(bf16[4,256,1024]{2,1,0:T(8,128)(2,1)} %up_ref.5) | copy-start | bytes 6291460
  14.3 31.0 %copy-start.5 = (bf16[4,256,128]{2,1,0:T(8,128)(2,1)S(1)}, bf16[4,256,128]{2,1,0:T(8,128)(2,1)}, u32[]{:S(2)}) copy-start(bf16[4,256,128]{2,1,0:T(8,128)(2,1)} %refs_0_.1) | copy-start | bytes 786436
  15.0 8.4 %collective-permute-start.4 = (bf16[4,256,128]{2,1,0:T(8,128)(2,1)S(1)}, bf16[4,256,128]{2,1,0:T(8,128)(2,1)S(1)}, u32[]{:S(2)}, u32[]{:S(2)}) collective-permute-start(bf16[4,256,128]{2,1,0:T(8,128)(2,1)S(1)} %shard_map.68.refs_0_), channel_id=1, source_target_pairs={{0,2},{1,3},{2,0},{3,1},{4,6},{5,7},{6,4},{7,5},{8,10},{9,11},{10,... | collective-permute-start | bytes 786440 | tf_op jit(solution)/shard_map/ppermute | solution.py:19
  16.8 6.6 %collective-permute-start.3 = (bf16[4,256,128]{2,1,0:T(8,128)(2,1)S(1)}, bf16[4,256,128]{2,1,0:T(8,128)(2,1)S(1)}, u32[]{:S(2)}, u32[]{:S(2)}) collective-permute-start(bf16[4,256,128]{2,1,0:T(8,128)(2,1)S(1)} %shard_map.68.refs_0_), channel_id=1, source_target_pairs={{0,1},{1,0},{2,3},{3,2},{4,5},{5,4},{6,7},{7,6},{8,9},{9,8},{10,11... | collective-permute-start | bytes 786440 | tf_op jit(solution)/shard_map/ppermute | solution.py:19
  23.4 1.5 collective-permute-start.5
  24.9 1.6 copy-start.3
  26.5 28.1 %copy-start.1 = (bf16[4,256,1024]{2,1,0:T(8,128)(2,1)S(1)}, bf16[4,256,1024]{2,1,0:T(8,128)(2,1)}, u32[]{:S(2)}) copy-start(bf16[4,256,1024]{2,1,0:T(8,128)(2,1)} %blocks_ref.7) | copy-start | bytes 6291460
  29.7 11.1 %collective-permute-start.6 = (bf16[4,256,128]{2,1,0:T(8,128)(2,1)S(1)}, bf16[4,256,128]{2,1,0:T(8,128)(2,1)S(1)}, u32[]{:S(2)}, u32[]{:S(2)}) collective-permute-start(bf16[4,256,128]{2,1,0:T(8,128)(2,1)S(1)} %get-tuple-element.14), channel_id=1, source_target_pairs={{0,4},{4,8},{8,12},{12,0},{1,5},{5,9},{9,13},{13,1},{2,6},{6,10},{... | collective-permute-start | bytes 786440 | tf_op jit(solution)/shard_map/ppermute | solution.py:24
  31.6 13.7 %collective-permute-start.7 = (bf16[4,256,128]{2,1,0:T(8,128)(2,1)S(1)}, bf16[4,256,128]{2,1,0:T(8,128)(2,1)S(1)}, u32[]{:S(2)}, u32[]{:S(2)}) collective-permute-start(bf16[4,256,128]{2,1,0:T(8,128)(2,1)S(1)} %get-tuple-element.15), channel_id=1, source_target_pairs={{0,12},{4,0},{8,4},{12,8},{1,13},{5,1},{9,5},{13,9},{2,14},{6,2},{... | collective-permute-start | bytes 786440 | tf_op jit(solution)/shard_map/ppermute | solution.py:24
  45.4 7.7 %collective-permute-start.9 = (bf16[4,256,128]{2,1,0:T(8,128)(2,1)S(1)}, bf16[4,256,128]{2,1,0:T(8,128)(2,1)S(1)}, u32[]{:S(2)}, u32[]{:S(2)}) collective-permute-start(bf16[4,256,128]{2,1,0:T(8,128)(2,1)S(1)} %fusion.refs_0_), channel_id=1, source_target_pairs={{0,2},{1,3},{2,0},{3,1},{4,6},{5,7},{6,4},{7,5},{8,10},{9,11},{10,... | collective-permute-start | bytes 786440 | tf_op jit(solution)/shard_map/ppermute | solution.py:19
  46.9 6.2 %collective-permute-start.8 = (bf16[4,256,128]{2,1,0:T(8,128)(2,1)S(1)}, bf16[4,256,128]{2,1,0:T(8,128)(2,1)S(1)}, u32[]{:S(2)}, u32[]{:S(2)}) collective-permute-start(bf16[4,256,128]{2,1,0:T(8,128)(2,1)S(1)} %fusion.refs_0_), channel_id=1, source_target_pairs={{0,1},{1,0},{2,3},{3,2},{4,5},{5,4},{6,7},{7,6},{8,9},{9,8},{10,11... | collective-permute-start | bytes 786440 | tf_op jit(solution)/shard_map/ppermute | solution.py:19
  53.1 1.5 collective-permute-start.10
  55.4 8.4 %collective-permute-start.12 = (bf16[4,256,128]{2,1,0:T(8,128)(2,1)S(1)}, bf16[4,256,128]{2,1,0:T(8,128)(2,1)S(1)}, u32[]{:S(2)}, u32[]{:S(2)}) collective-permute-start(bf16[4,256,128]{2,1,0:T(8,128)(2,1)S(1)} %shard_map.70.refs_0_), channel_id=1, source_target_pairs={{0,2},{1,3},{2,0},{3,1},{4,6},{5,7},{6,4},{7,5},{8,10},{9,11},{10,... | collective-permute-start | bytes 786440 | tf_op jit(solution)/shard_map/ppermute | solution.py:19
  56.9 6.9 %collective-permute-start.11 = (bf16[4,256,128]{2,1,0:T(8,128)(2,1)S(1)}, bf16[4,256,128]{2,1,0:T(8,128)(2,1)S(1)}, u32[]{:S(2)}, u32[]{:S(2)}) collective-permute-start(bf16[4,256,128]{2,1,0:T(8,128)(2,1)S(1)} %shard_map.70.refs_0_), channel_id=1, source_target_pairs={{0,1},{1,0},{2,3},{3,2},{4,5},{5,4},{6,7},{7,6},{8,9},{9,8},{10,11... | collective-permute-start | bytes 786440 | tf_op jit(solution)/shard_map/ppermute | solution.py:19
  63.8 1.5 collective-permute-start.13
  68.4 11.1 %collective-permute-start.14 = (bf16[4,256,128]{2,1,0:T(8,128)(2,1)S(1)}, bf16[4,256,128]{2,1,0:T(8,128)(2,1)S(1)}, u32[]{:S(2)}, u32[]{:S(2)}) collective-permute-start(bf16[4,256,128]{2,1,0:T(8,128)(2,1)S(1)} %get-tuple-element.17), channel_id=1, source_target_pairs={{0,4},{4,8},{8,12},{12,0},{1,5},{5,9},{9,13},{13,1},{2,6},{6,10},{... | collective-permute-start | bytes 786440 | tf_op jit(solution)/shard_map/ppermute | solution.py:24
  70.2 13.7 %collective-permute-start.15 = (bf16[4,256,128]{2,1,0:T(8,128)(2,1)S(1)}, bf16[4,256,128]{2,1,0:T(8,128)(2,1)S(1)}, u32[]{:S(2)}, u32[]{:S(2)}) collective-permute-start(bf16[4,256,128]{2,1,0:T(8,128)(2,1)S(1)} %get-tuple-element.18), channel_id=1, source_target_pairs={{0,12},{4,0},{8,4},{12,8},{1,13},{5,1},{9,5},{13,9},{2,14},{6,2},{... | collective-permute-start | bytes 786440 | tf_op jit(solution)/shard_map/ppermute | solution.py:24
  84.0 7.9 %collective-permute-start.17 = (bf16[4,256,128]{2,1,0:T(8,128)(2,1)S(1)}, bf16[4,256,128]{2,1,0:T(8,128)(2,1)S(1)}, u32[]{:S(2)}, u32[]{:S(2)}) collective-permute-start(bf16[4,256,128]{2,1,0:T(8,128)(2,1)S(1)} %fusion.1.refs_0_), channel_id=1, source_target_pairs={{0,2},{1,3},{2,0},{3,1},{4,6},{5,7},{6,4},{7,5},{8,10},{9,11},{10,... | collective-permute-start | bytes 786440 | tf_op jit(solution)/shard_map/ppermute | solution.py:19
  85.5 6.4 %collective-permute-start.16 = (bf16[4,256,128]{2,1,0:T(8,128)(2,1)S(1)}, bf16[4,256,128]{2,1,0:T(8,128)(2,1)S(1)}, u32[]{:S(2)}, u32[]{:S(2)}) collective-permute-start(bf16[4,256,128]{2,1,0:T(8,128)(2,1)S(1)} %fusion.1.refs_0_), channel_id=1, source_target_pairs={{0,1},{1,0},{2,3},{3,2},{4,5},{5,4},{6,7},{7,6},{8,9},{9,8},{10,11... | collective-permute-start | bytes 786440 | tf_op jit(solution)/shard_map/ppermute | solution.py:19
  91.9 1.5 collective-permute-start.18
  94.2 8.4 %collective-permute-start.20 = (bf16[4,256,128]{2,1,0:T(8,128)(2,1)S(1)}, bf16[4,256,128]{2,1,0:T(8,128)(2,1)S(1)}, u32[]{:S(2)}, u32[]{:S(2)}) collective-permute-start(bf16[4,256,128]{2,1,0:T(8,128)(2,1)S(1)} %shard_map.72.refs_0_), channel_id=1, source_target_pairs={{0,2},{1,3},{2,0},{3,1},{4,6},{5,7},{6,4},{7,5},{8,10},{9,11},{10,... | collective-permute-start | bytes 786440 | tf_op jit(solution)/shard_map/ppermute | solution.py:19
  95.7 6.9 %collective-permute-start.19 = (bf16[4,256,128]{2,1,0:T(8,128)(2,1)S(1)}, bf16[4,256,128]{2,1,0:T(8,128)(2,1)S(1)}, u32[]{:S(2)}, u32[]{:S(2)}) collective-permute-start(bf16[4,256,128]{2,1,0:T(8,128)(2,1)S(1)} %shard_map.72.refs_0_), channel_id=1, source_target_pairs={{0,1},{1,0},{2,3},{3,2},{4,5},{5,4},{6,7},{7,6},{8,9},{9,8},{10,11... | collective-permute-start | bytes 786440 | tf_op jit(solution)/shard_map/ppermute | solution.py:19
  102.6 1.5 collective-permute-start.21
  107.2 11.1 %collective-permute-start.22 = (bf16[4,256,128]{2,1,0:T(8,128)(2,1)S(1)}, bf16[4,256,128]{2,1,0:T(8,128)(2,1)S(1)}, u32[]{:S(2)}, u32[]{:S(2)}) collective-permute-start(bf16[4,256,128]{2,1,0:T(8,128)(2,1)S(1)} %get-tuple-element.20), channel_id=1, source_target_pairs={{0,4},{4,8},{8,12},{12,0},{1,5},{5,9},{9,13},{13,1},{2,6},{6,10},{... | collective-permute-start | bytes 786440 | tf_op jit(solution)/shard_map/ppermute | solution.py:24
  107.4 14.1 %collective-permute-start.23 = (bf16[4,256,128]{2,1,0:T(8,128)(2,1)S(1)}, bf16[4,256,128]{2,1,0:T(8,128)(2,1)S(1)}, u32[]{:S(2)}, u32[]{:S(2)}) collective-permute-start(bf16[4,256,128]{2,1,0:T(8,128)(2,1)S(1)} %get-tuple-element.21), channel_id=1, source_target_pairs={{0,12},{4,0},{8,4},{12,8},{1,13},{5,1},{9,5},{13,9},{2,14},{6,2},{... | collective-permute-start | bytes 786440 | tf_op jit(solution)/shard_map/ppermute | solution.py:24
  121.7 7.6 %collective-permute-start.25 = (bf16[4,256,128]{2,1,0:T(8,128)(2,1)S(1)}, bf16[4,256,128]{2,1,0:T(8,128)(2,1)S(1)}, u32[]{:S(2)}, u32[]{:S(2)}) collective-permute-start(bf16[4,256,128]{2,1,0:T(8,128)(2,1)S(1)} %fusion.2.refs_0_), channel_id=1, source_target_pairs={{0,2},{1,3},{2,0},{3,1},{4,6},{5,7},{6,4},{7,5},{8,10},{9,11},{10,... | collective-permute-start | bytes 786440 | tf_op jit(solution)/shard_map/ppermute | solution.py:19
  123.1 6.1 %collective-permute-start.24 = (bf16[4,256,128]{2,1,0:T(8,128)(2,1)S(1)}, bf16[4,256,128]{2,1,0:T(8,128)(2,1)S(1)}, u32[]{:S(2)}, u32[]{:S(2)}) collective-permute-start(bf16[4,256,128]{2,1,0:T(8,128)(2,1)S(1)} %fusion.2.refs_0_), channel_id=1, source_target_pairs={{0,1},{1,0},{2,3},{3,2},{4,5},{5,4},{6,7},{7,6},{8,9},{9,8},{10,11... | collective-permute-start | bytes 786440 | tf_op jit(solution)/shard_map/ppermute | solution.py:19
  129.2 1.5 collective-permute-start.26
  132.5 1.3 collective-permute-start.27
  133.9 4.3 %collective-permute-start.28 = (f32[128,128]{0,1:T(8,128)S(1)}, f32[128,128]{0,1:T(8,128)S(1)}, u32[]{:S(2)}, u32[]{:S(2)}) collective-permute-start(f32[128,128]{0,1:T(8,128)S(1)} %add.48), channel_id=1, source_target_pairs={{0,2},{1,3},{2,0},{3,1},{4,6},{5,7},{6,4},{7,5},{8,10},{9,11},{10,... | collective-permute-start | bytes 196616 | tf_op jit(solution)/shard_map/ppermute | solution.py:19
  138.2 4.3 %collective-permute-start.29 = (f32[128,128]{0,1:T(8,128)S(1)}, f32[128,128]{0,1:T(8,128)S(1)}, u32[]{:S(2)}, u32[]{:S(2)}) collective-permute-start(f32[128,128]{0,1:T(8,128)S(1)} %add.49), channel_id=1, source_target_pairs={{0,4},{4,0},{8,12},{12,8},{1,5},{5,1},{9,13},{13,9},{2,6},{6,2},{1... | collective-permute-start | bytes 196616 | tf_op jit(solution)/shard_map/ppermute | solution.py:19
  142.5 5.8 %collective-permute-start.30 = (f32[128,128]{0,1:T(8,128)S(1)}, f32[128,128]{0,1:T(8,128)S(1)}, u32[]{:S(2)}, u32[]{:S(2)}) collective-permute-start(f32[128,128]{0,1:T(8,128)S(1)} %add.50), channel_id=1, source_target_pairs={{0,8},{4,12},{8,0},{12,4},{1,9},{5,13},{9,1},{13,5},{2,10},{6,14},... | collective-permute-start | bytes 196616 | tf_op jit(solution)/shard_map/ppermute | solution.py:19

commit v2 on v1

--- a/solution.py
+++ b/solution.py
@@ -9,6 +9,7 @@
 
 BAND = 4
 SWEEPS = 3
+SUB = 8
 F32 = jnp.float32
 BF16 = jnp.bfloat16
 VMEM = pl.BlockSpec(memory_space=pltpu.VMEM)
@@ -136,6 +137,76 @@
     return value
 
 
+def spread(row, height):
+    return jnp.broadcast_to(row, (height, row.shape[1]))
+
+
+def factor(gram):
+    size = gram.shape[0]
+    panels = size // SUB
+    level = lax.broadcasted_iota(jnp.int32, (SUB, size), 0)
+    lane = lax.broadcasted_iota(jnp.int32, (SUB, size), 1)
+    upper = [gram[SUB * p : SUB * (p + 1)] for p in range(panels)]
+    inverse = [jnp.where(lane == level + SUB * p, 1.0, 0.0) for p in range(panels)]
+    for p in range(panels):
+        column = {
+            q: [
+                jnp.broadcast_to(upper[q][:, SUB * p + j : SUB * p + j + 1], (SUB, size))
+                for j in range(SUB)
+            ]
+            for q in range(p, panels)
+        }
+        for k in range(SUB):
+            scale = lax.rsqrt(spread(column[p][k][k : k + 1], SUB))
+            heads = [spread(column[p][j][k : k + 1], SUB) * scale for j in range(k + 1, SUB)]
+            row = spread(upper[p][k : k + 1], SUB) * scale
+            back = spread(inverse[p][k : k + 1], SUB) * scale
+            for q in range(p, panels):
+                part = column[q][k] * scale
+                if q == p:
+                    part = jnp.where(level > k, part, 0.0)
+                for j, head in enumerate(heads):
+                    column[q][k + 1 + j] -= part * head
+                upper[q] -= part * row
+                inverse[q] -= part * back
+            upper[p] = jnp.where(level == k, row, upper[p])
+            inverse[p] = jnp.where(level == k, back, inverse[p])
+    for p in range(panels):
+        upper[p] = jnp.where(lane >= level + SUB * p, upper[p], 0.0)
+        inverse[p] = jnp.where(lane <= level + SUB * p, inverse[p], 0.0)
+    return upper, inverse
+
+
+def basis_kernel(entries, gram_ref, sampled_ref, basis_ref, triangle_ref, inverse_ref):
+    upper, inverse = factor(gram_ref[...] / entries)
+    for p, rows in enumerate(upper):
+        triangle_ref[SUB * p : SUB * (p + 1)] = rows
+    for p, rows in enumerate(inverse):
+        inverse_ref[SUB * p : SUB * (p + 1)] = rows
+    for h in range(sampled_ref.shape[0]):
+        basis_ref[h] = lax.dot_general(
+            sampled_ref[h],
+            inverse_ref[...],
+            (((1,), (1,)), ((), ())),
+            precision=lax.Precision.HIGHEST,
+            preferred_element_type=F32,
+        )
+
+
+def basis_of(gram, sampled, entries):
+    return pl.pallas_call(
+        functools.partial(basis_kernel, entries),
+        out_shape=[
+            jax.ShapeDtypeStruct(sampled.shape, F32),
+            jax.ShapeDtypeStruct(gram.shape, F32),
+        ],
+        in_specs=[VMEM, VMEM],
+        out_specs=[VMEM, VMEM],
+        scratch_shapes=[pltpu.VMEM(gram.shape, F32)],
+        compiler_params=params(12),
+    )(gram, sampled)
+
+
 def body(sketch, inverse_blocks, couple_up, couple_down, strip_harmonics):
     count, rows, width = sketch.shape
     place = lax.axis_index("wall").astype(jnp.int32).reshape(1)
@@ -154,11 +225,7 @@
         else:
             sampled, gram = apply_inverse(place, inverse_blocks, rhs, True)
     entries = lax.axis_size("harm") * lax.axis_size("wall") * count * rows
-    gram = all_sum(gram) / entries
-    lower = jnp.linalg.cholesky(gram)
-    flat = sampled.reshape(count * rows, width)
-    basis = jax.scipy.linalg.solve_triangular(lower, flat.T, lower=True).T
-    return (basis.reshape(count, rows, width), lower.T)
+    return tuple(basis_of(all_sum(gram), sampled, entries))
 
 
 def solution(mesh):

time: 174 us -> 154 us (0.89)
  other arithmetic: 23.3 us -> 0.41 us
  Pallas kernels: 13.2 us -> 18.7 us
    another operation x4 -> x0, other arithmetic: 22.2 us -> none  [the longest x3 12.4 us: body(): lower = jnp.linalg.cholesky(gram)]
    pallas_call x0 -> x1, Pallas kernels: none -> 5.52 us  [basis_of(): pl.pallas_call(functools.partial(basis_kernel, entries), out_shape=[jax.S...]
    unnamed x15 -> x14, local copies, waits for them, and re-layouts: 4.88 us -> 4.15 us
where the time goes in v2:
time: 154 us
  waiting for transfers between devices  101 us (66%)
  starting transfers between devices  28.8 us (19%)
  Pallas kernels  18.7 us (12%)
  local copies, waits for them, and re-layouts  4.15 us (3%)
    ppermute x25, waiting for transfers between devices, flip(): lax.ppermute(value, axis, [(i, i ^ mask) for i in range(lax.axis_size(axi...  67.4 us
    ppermute x6, waiting for transfers between devices, turn(): lax.ppermute(value, axis, [(i, (i + step) % count) for i in range(count)])  33.6 us
    ppermute x25, starting transfers between devices, flip(): lax.ppermute(value, axis, [(i, i ^ mask) for i in range(lax.axis_size(axi...  17.1 us
    ppermute x6, starting transfers between devices, turn(): lax.ppermute(value, axis, [(i, (i + step) % count) for i in range(count)])  11.7 us
    pallas_call x3, Pallas kernels, couple(): pl.pallas_call(functools.partial(couple_kernel, len(pieces)), out_shape=[...  9.4 us
    pallas_call x1, Pallas kernels, basis_of(): pl.pallas_call(functools.partial(basis_kernel, entries), out_shape=[jax.S...  5.52 us
    unnamed x14, local copies, waits for them, and re-layouts  4.15 us
    pallas_call x4, Pallas kernels, apply_inverse(): pl.pallas_call(functools.partial(inverse_kernel, len(pieces), last), out_...  3.76 us
  transfers between devices with their start and end apart: 31, of which 24 were waited for; matrix products, arithmetic and copies ran while one was open for 0% of the time, Pallas kernels for 0%

profile of v2, /device:TPU:0, one launch (start us, length us, event | category | flops | bytes accessed | tf_op | source)
XLA Modules:
  0.0 153.8 jit_solution(1203091891915165489)
XLA Ops:
  0.6 3.0 %collective-permute-start.1 = (bf16[4,256,128]{2,1,0:T(8,128)(2,1)}, bf16[4,256,128]{2,1,0:T(8,128)(2,1)S(1)}, u32[]{:S(2)}, u32[]{:S(2)}) collective-permute-start(bf16[4,256,128]{2,1,0:T(8,128)(2,1)} %refs_0_.1), channel_id=1, source_target_pairs={{0,2},{1,3},{2,0},{3,1},{4,6},{5,7},{6,4},{7,5},{8,10},{9,11},{10,... | collective-permute-start | bytes 786440 | tf_op jit(solution)/shard_map/ppermute | solution.py:20
  3.7 6.5 %collective-permute-done.1.refs_2_ = bf16[4,256,128]{2,1,0:T(8,128)(2,1)S(1)} collective-permute-done((bf16[4,256,128]{2,1,0:T(8,128)(2,1)}, bf16[4,256,128]{2,1,0:T(8,128)(2,1)S(1)}, u32[]{:S(2)}, u32[]{:S(2)}) %collective-permute-start.1) | collective-permute-done | bytes 262176 | tf_op jit(solution)/shard_map/ppermute | solution.py:20
  10.2 1.5 collective-permute-done.2.refs_3_
  11.7 1.6 %copy-done = bf16[4,256,1024]{2,1,0:T(8,128)(2,1)S(1)} copy-done((bf16[4,256,1024]{2,1,0:T(8,128)(2,1)S(1)}, bf16[4,256,1024]{2,1,0:T(8,128)(2,1)}, u32[]{:S(2)}) %copy-start) | copy-done | bytes 2097176
  13.3 0.9 copy-done.4
  15.0 1.8 %collective-permute-start.4 = (bf16[4,256,128]{2,1,0:T(8,128)(2,1)S(1)}, bf16[4,256,128]{2,1,0:T(8,128)(2,1)S(1)}, u32[]{:S(2)}, u32[]{:S(2)}) collective-permute-start(bf16[4,256,128]{2,1,0:T(8,128)(2,1)S(1)} %shard_map.68.refs_0_), channel_id=1, source_target_pairs={{0,2},{1,3},{2,0},{3,1},{4,6},{5,7},{6,4},{7,5},{8,10},{9,11},{10,... | collective-permute-start | bytes 786440 | tf_op jit(solution)/shard_map/ppermute | solution.py:20
  16.8 6.6 %collective-permute-done.4.refs_2_ = bf16[4,256,128]{2,1,0:T(8,128)(2,1)S(1)} collective-permute-done((bf16[4,256,128]{2,1,0:T(8,128)(2,1)S(1)}, bf16[4,256,128]{2,1,0:T(8,128)(2,1)S(1)}, u32[]{:S(2)}, u32[]{:S(2)}) %collective-permute-start.4) | collective-permute-done | bytes 262176 | tf_op jit(solution)/shard_map/ppermute | solution.py:20
  23.4 1.5 collective-permute-done.5.refs_3_
  24.9 1.6 %copy-done.3 = bf16[4,256,1024]{2,1,0:T(8,128)(2,1)S(1)} copy-done((bf16[4,256,1024]{2,1,0:T(8,128)(2,1)S(1)}, bf16[4,256,1024]{2,1,0:T(8,128)(2,1)}, u32[]{:S(2)}) %copy-start.3) | copy-done | bytes 2097176
  26.5 3.1 %shard_map.69 = (f32[4,256,128]{2,1,0:T(8,128)S(1)}, bf16[4,256,128]{2,1,0:T(8,128)(2,1)S(1)}, bf16[4,256,128]{2,1,0:T(8,128)(2,1)S(1)}) custom-call(s32[1]{0:T(128)} %bitcast.place_ref, s32[4]{0:T(128)S(1)} %copy-done.6, bf16[4,256,1024]{2,1,0:T(8,128)(2,1)S(1)} %copy-done.2, bf16[4,256,1024]{2,1,0:T(8,128)(2,1)S(1)} %copy-done.3, ...), custom_call_target="tpu_custom_call" | custom-call | tf_op jit(solution)/shard_map/pallas_call | solution.py:114
  29.7 1.9 %collective-permute-start.6 = (bf16[4,256,128]{2,1,0:T(8,128)(2,1)S(1)}, bf16[4,256,128]{2,1,0:T(8,128)(2,1)S(1)}, u32[]{:S(2)}, u32[]{:S(2)}) collective-permute-start(bf16[4,256,128]{2,1,0:T(8,128)(2,1)S(1)} %get-tuple-element.14), channel_id=1, source_target_pairs={{0,4},{4,8},{8,12},{12,0},{1,5},{5,9},{9,13},{13,1},{2,6},{6,10},{... | collective-permute-start | bytes 786440 | tf_op jit(solution)/shard_map/ppermute | solution.py:25
  31.6 2.1 %collective-permute-start.7 = (bf16[4,256,128]{2,1,0:T(8,128)(2,1)S(1)}, bf16[4,256,128]{2,1,0:T(8,128)(2,1)S(1)}, u32[]{:S(2)}, u32[]{:S(2)}) collective-permute-start(bf16[4,256,128]{2,1,0:T(8,128)(2,1)S(1)} %get-tuple-element.15), channel_id=1, source_target_pairs={{0,12},{4,0},{8,4},{12,8},{1,13},{5,1},{9,5},{13,9},{2,14},{6,2},{... | collective-permute-start | bytes 786440 | tf_op jit(solution)/shard_map/ppermute | solution.py:25
  33.7 7.1 %collective-permute-done.6 = bf16[4,256,128]{2,1,0:T(8,128)(2,1)S(1)} collective-permute-done((bf16[4,256,128]{2,1,0:T(8,128)(2,1)S(1)}, bf16[4,256,128]{2,1,0:T(8,128)(2,1)S(1)}, u32[]{:S(2)}, u32[]{:S(2)}) %collective-permute-start.6) | collective-permute-done | bytes 262176 | tf_op jit(solution)/shard_map/ppermute | solution.py:25
  40.8 4.5 %collective-permute-done.7 = bf16[4,256,128]{2,1,0:T(8,128)(2,1)S(1)} collective-permute-done((bf16[4,256,128]{2,1,0:T(8,128)(2,1)S(1)}, bf16[4,256,128]{2,1,0:T(8,128)(2,1)S(1)}, u32[]{:S(2)}, u32[]{:S(2)}) %collective-permute-start.7) | collective-permute-done | bytes 262176 | tf_op jit(solution)/shard_map/ppermute | solution.py:25
  45.4 1.5 collective-permute-start.9
  46.9 6.2 %collective-permute-done.9.refs_2_ = bf16[4,256,128]{2,1,0:T(8,128)(2,1)S(1)} collective-permute-done((bf16[4,256,128]{2,1,0:T(8,128)(2,1)S(1)}, bf16[4,256,128]{2,1,0:T(8,128)(2,1)S(1)}, u32[]{:S(2)}, u32[]{:S(2)}) %collective-permute-start.9) | collective-permute-done | bytes 262176 | tf_op jit(solution)/shard_map/ppermute | solution.py:20
  53.1 1.5 collective-permute-done.10.refs_3_
  54.7 0.7 shard_map.70.refs_0_
  55.4 1.5 collective-permute-start.12
  56.9 6.9 %collective-permute-done.12.refs_2_ = bf16[4,256,128]{2,1,0:T(8,128)(2,1)S(1)} collective-permute-done((bf16[4,256,128]{2,1,0:T(8,128)(2,1)S(1)}, bf16[4,256,128]{2,1,0:T(8,128)(2,1)S(1)}, u32[]{:S(2)}, u32[]{:S(2)}) %collective-permute-start.12) | collective-permute-done | bytes 262176 | tf_op jit(solution)/shard_map/ppermute | solution.py:20
  63.8 1.5 collective-permute-done.13.refs_3_
  65.3 3.1 %shard_map.71 = (f32[4,256,128]{2,1,0:T(8,128)S(1)}, bf16[4,256,128]{2,1,0:T(8,128)(2,1)S(1)}, bf16[4,256,128]{2,1,0:T(8,128)(2,1)S(1)}) custom-call(s32[1]{0:T(128)} %bitcast.place_ref, s32[4]{0:T(128)S(1)} %copy-done.6, bf16[4,256,1024]{2,1,0:T(8,128)(2,1)S(1)} %copy-done.2, bf16[4,256,1024]{2,1,0:T(8,128)(2,1)S(1)} %copy-done.3, ...), custom_call_target="tpu_custom_call" | custom-call | tf_op jit(solution)/shard_map/pallas_call | solution.py:114
  68.4 1.7 %collective-permute-start.14 = (bf16[4,256,128]{2,1,0:T(8,128)(2,1)S(1)}, bf16[4,256,128]{2,1,0:T(8,128)(2,1)S(1)}, u32[]{:S(2)}, u32[]{:S(2)}) collective-permute-start(bf16[4,256,128]{2,1,0:T(8,128)(2,1)S(1)} %get-tuple-element.17), channel_id=1, source_target_pairs={{0,4},{4,8},{8,12},{12,0},{1,5},{5,9},{9,13},{13,1},{2,6},{6,10},{... | collective-permute-start | bytes 786440 | tf_op jit(solution)/shard_map/ppermute | solution.py:25
  70.2 2.1 %collective-permute-start.15 = (bf16[4,256,128]{2,1,0:T(8,128)(2,1)S(1)}, bf16[4,256,128]{2,1,0:T(8,128)(2,1)S(1)}, u32[]{:S(2)}, u32[]{:S(2)}) collective-permute-start(bf16[4,256,128]{2,1,0:T(8,128)(2,1)S(1)} %get-tuple-element.18), channel_id=1, source_target_pairs={{0,12},{4,0},{8,4},{12,8},{1,13},{5,1},{9,5},{13,9},{2,14},{6,2},{... | collective-permute-start | bytes 786440 | tf_op jit(solution)/shard_map/ppermute | solution.py:25
  72.3 7.2 %collective-permute-done.14 = bf16[4,256,128]{2,1,0:T(8,128)(2,1)S(1)} collective-permute-done((bf16[4,256,128]{2,1,0:T(8,128)(2,1)S(1)}, bf16[4,256,128]{2,1,0:T(8,128)(2,1)S(1)}, u32[]{:S(2)}, u32[]{:S(2)}) %collective-permute-start.14) | collective-permute-done | bytes 262176 | tf_op jit(solution)/shard_map/ppermute | solution.py:25
  79.5 4.4 %collective-permute-done.15 = bf16[4,256,128]{2,1,0:T(8,128)(2,1)S(1)} collective-permute-done((bf16[4,256,128]{2,1,0:T(8,128)(2,1)S(1)}, bf16[4,256,128]{2,1,0:T(8,128)(2,1)S(1)}, u32[]{:S(2)}, u32[]{:S(2)}) %collective-permute-start.15) | collective-permute-done | bytes 262176 | tf_op jit(solution)/shard_map/ppermute | solution.py:25
  84.0 1.5 collective-permute-start.17
  85.5 6.4 %collective-permute-done.17.refs_2_ = bf16[4,256,128]{2,1,0:T(8,128)(2,1)S(1)} collective-permute-done((bf16[4,256,128]{2,1,0:T(8,128)(2,1)S(1)}, bf16[4,256,128]{2,1,0:T(8,128)(2,1)S(1)}, u32[]{:S(2)}, u32[]{:S(2)}) %collective-permute-start.17) | collective-permute-done | bytes 262176 | tf_op jit(solution)/shard_map/ppermute | solution.py:20
  91.9 1.5 collective-permute-done.18.refs_3_
  93.5 0.7 shard_map.72.refs_0_
  94.2 1.5 collective-permute-start.20
  95.7 6.9 %collective-permute-done.20.refs_2_ = bf16[4,256,128]{2,1,0:T(8,128)(2,1)S(1)} collective-permute-done((bf16[4,256,128]{2,1,0:T(8,128)(2,1)S(1)}, bf16[4,256,128]{2,1,0:T(8,128)(2,1)S(1)}, u32[]{:S(2)}, u32[]{:S(2)}) %collective-permute-start.20) | collective-permute-done | bytes 262176 | tf_op jit(solution)/shard_map/ppermute | solution.py:20
  102.6 1.5 collective-permute-done.21.refs_3_
  104.1 3.1 %shard_map.73 = (f32[4,256,128]{2,1,0:T(8,128)S(1)}, bf16[4,256,128]{2,1,0:T(8,128)(2,1)S(1)}, bf16[4,256,128]{2,1,0:T(8,128)(2,1)S(1)}) custom-call(s32[1]{0:T(128)} %bitcast.place_ref, s32[4]{0:T(128)S(1)} %copy-done.6, bf16[4,256,1024]{2,1,0:T(8,128)(2,1)S(1)} %copy-done.2, bf16[4,256,1024]{2,1,0:T(8,128)(2,1)S(1)} %copy-done.3, ...), custom_call_target="tpu_custom_call" | custom-call | tf_op jit(solution)/shard_map/pallas_call | solution.py:114
  107.4 3.7 %collective-permute-start.23 = (bf16[4,256,128]{2,1,0:T(8,128)(2,1)S(1)}, bf16[4,256,128]{2,1,0:T(8,128)(2,1)S(1)}, u32[]{:S(2)}, u32[]{:S(2)}) collective-permute-start(bf16[4,256,128]{2,1,0:T(8,128)(2,1)S(1)} %get-tuple-element.21), channel_id=1, source_target_pairs={{0,12},{4,0},{8,4},{12,8},{1,13},{5,1},{9,5},{13,9},{2,14},{6,2},{... | collective-permute-start | bytes 786440 | tf_op jit(solution)/shard_map/ppermute | solution.py:25
  111.1 7.2 %collective-permute-done.22 = bf16[4,256,128]{2,1,0:T(8,128)(2,1)S(1)} collective-permute-done((bf16[4,256,128]{2,1,0:T(8,128)(2,1)S(1)}, bf16[4,256,128]{2,1,0:T(8,128)(2,1)S(1)}, u32[]{:S(2)}, u32[]{:S(2)}) %collective-permute-start.22) | collective-permute-done | bytes 262176 | tf_op jit(solution)/shard_map/ppermute | solution.py:25
  118.3 3.2 %collective-permute-done.23 = bf16[4,256,128]{2,1,0:T(8,128)(2,1)S(1)} collective-permute-done((bf16[4,256,128]{2,1,0:T(8,128)(2,1)S(1)}, bf16[4,256,128]{2,1,0:T(8,128)(2,1)S(1)}, u32[]{:S(2)}, u32[]{:S(2)}) %collective-permute-start.23) | collective-permute-done | bytes 262176 | tf_op jit(solution)/shard_map/ppermute | solution.py:25
  121.7 1.5 collective-permute-start.25
  123.1 6.1 %collective-permute-done.25.refs_2_ = bf16[4,256,128]{2,1,0:T(8,128)(2,1)S(1)} collective-permute-done((bf16[4,256,128]{2,1,0:T(8,128)(2,1)S(1)}, bf16[4,256,128]{2,1,0:T(8,128)(2,1)S(1)}, u32[]{:S(2)}, u32[]{:S(2)}) %collective-permute-start.25) | collective-permute-done | bytes 262176 | tf_op jit(solution)/shard_map/ppermute | solution.py:20
  129.2 1.5 collective-permute-done.26.refs_3_
  130.8 1.6 %shard_map.74 = (f32[4,256,128]{2,1,0:T(8,128)S(1)}, f32[128,128]{1,0:T(8,128)S(1)}) custom-call(s32[1]{0:T(128)} %bitcast.place_ref, bf16[4,256,1024]{2,1,0:T(8,128)(2,1)S(1)} %copy-done.1, bf16[4,256,128]{2,1,0:T(8,128)(2,1)S(1)} %fusion.2.refs_0_, bf16[4,256,128]{2,1,0:T(8,128)(2,1)S(1)} %collective-permute-done.24.refs_1_, ...), custom_call_target="tpu_custom_call" | custom-call | tf_op jit(solution)/shard_map/pallas_call | solution.py:78
  132.6 1.1 collective-permute-done.27
  133.8 1.5 collective-permute-start.28
  135.2 2.9 %collective-permute-done.28 = f32[128,128]{1,0:T(8,128)S(1)} collective-permute-done((f32[128,128]{1,0:T(8,128)S(1)}, f32[128,128]{1,0:T(8,128)S(1)}, u32[]{:S(2)}, u32[]{:S(2)}) %collective-permute-start.28) | collective-permute-done | bytes 65568 | tf_op jit(solution)/shard_map/ppermute | solution.py:20
  138.6 3.8 %collective-permute-done.29 = f32[128,128]{1,0:T(8,128)S(1)} collective-permute-done((f32[128,128]{1,0:T(8,128)S(1)}, f32[128,128]{1,0:T(8,128)S(1)}, u32[]{:S(2)}, u32[]{:S(2)}) %collective-permute-start.29) | collective-permute-done | bytes 65568 | tf_op jit(solution)/shard_map/ppermute | solution.py:20
  142.4 2.5 %collective-permute-start.30 = (f32[128,128]{1,0:T(8,128)S(1)}, f32[128,128]{1,0:T(8,128)S(1)}, u32[]{:S(2)}, u32[]{:S(2)}) collective-permute-start(f32[128,128]{1,0:T(8,128)S(1)} %add.38), channel_id=1, source_target_pairs={{0,8},{4,12},{8,0},{12,4},{1,9},{5,13},{9,1},{13,5},{2,10},{6,14},... | collective-permute-start | bytes 196616 | tf_op jit(solution)/shard_map/ppermute | solution.py:20
  145.0 3.3 %collective-permute-done.30 = f32[128,128]{1,0:T(8,128)S(1)} collective-permute-done((f32[128,128]{1,0:T(8,128)S(1)}, f32[128,128]{1,0:T(8,128)S(1)}, u32[]{:S(2)}, u32[]{:S(2)}) %collective-permute-start.30) | collective-permute-done | bytes 65568 | tf_op jit(solution)/shard_map/ppermute | solution.py:20
  148.3 5.5 %shard_map.75 = (f32[4,256,128]{2,1,0:T(8,128)}, f32[128,128]{1,0:T(8,128)}) custom-call(f32[128,128]{1,0:T(8,128)S(1)} %add.39.gram_ref, f32[4,256,128]{2,1,0:T(8,128)S(1)} %get-tuple-element.23.sampled_ref), custom_call_target="tpu_custom_call" | custom-call | tf_op jit(solution)/shard_map/pallas_call | solution.py:197
  (43 shorter events, 2.1 us)
Async XLA Ops:
  0.6 24.3 %copy-start.6 = (s32[4]{0:T(128)S(1)}, s32[4]{0:T(128)}, u32[]{:S(2)}) copy-start(s32[4]{0:T(128)} %strip_ref.5) | copy-start | bytes 52
  0.6 9.5 %collective-permute-start.1 = (bf16[4,256,128]{2,1,0:T(8,128)(2,1)}, bf16[4,256,128]{2,1,0:T(8,128)(2,1)S(1)}, u32[]{:S(2)}, u32[]{:S(2)}) collective-permute-start(bf16[4,256,128]{2,1,0:T(8,128)(2,1)} %refs_0_.1), channel_id=1, source_target_pairs={{0,2},{1,3},{2,0},{3,1},{4,6},{5,7},{6,4},{7,5},{8,10},{9,11},{10,... | collective-permute-start | bytes 786440 | tf_op jit(solution)/shard_map/ppermute | solution.py:20
  3.7 6.5 %collective-permute-start = (bf16[4,256,128]{2,1,0:T(8,128)(2,1)}, bf16[4,256,128]{2,1,0:T(8,128)(2,1)S(1)}, u32[]{:S(2)}, u32[]{:S(2)}) collective-permute-start(bf16[4,256,128]{2,1,0:T(8,128)(2,1)} %refs_0_.1), channel_id=1, source_target_pairs={{0,1},{1,0},{2,3},{3,2},{4,5},{5,4},{6,7},{7,6},{8,9},{9,8},{10,11... | collective-permute-start | bytes 786440 | tf_op jit(solution)/shard_map/ppermute | solution.py:20
  10.2 1.5 collective-permute-start.2
  11.7 1.6 %copy-start = (bf16[4,256,1024]{2,1,0:T(8,128)(2,1)S(1)}, bf16[4,256,1024]{2,1,0:T(8,128)(2,1)}, u32[]{:S(2)}) copy-start(bf16[4,256,1024]{2,1,0:T(8,128)(2,1)} %blocks_ref.7) | copy-start | bytes 6291460
  13.3 0.9 copy-start.4
  14.3 10.7 %copy-start.2 = (bf16[4,256,1024]{2,1,0:T(8,128)(2,1)S(1)}, bf16[4,256,1024]{2,1,0:T(8,128)(2,1)}, u32[]{:S(2)}) copy-start(bf16[4,256,1024]{2,1,0:T(8,128)(2,1)} %up_ref.5) | copy-start | bytes 6291460
  14.3 31.0 %copy-start.5 = (bf16[4,256,128]{2,1,0:T(8,128)(2,1)S(1)}, bf16[4,256,128]{2,1,0:T(8,128)(2,1)}, u32[]{:S(2)}) copy-start(bf16[4,256,128]{2,1,0:T(8,128)(2,1)} %refs_0_.1) | copy-start | bytes 786436
  15.0 8.4 %collective-permute-start.4 = (bf16[4,256,128]{2,1,0:T(8,128)(2,1)S(1)}, bf16[4,256,128]{2,1,0:T(8,128)(2,1)S(1)}, u32[]{:S(2)}, u32[]{:S(2)}) collective-permute-start(bf16[4,256,128]{2,1,0:T(8,128)(2,1)S(1)} %shard_map.68.refs_0_), channel_id=1, source_target_pairs={{0,2},{1,3},{2,0},{3,1},{4,6},{5,7},{6,4},{7,5},{8,10},{9,11},{10,... | collective-permute-start | bytes 786440 | tf_op jit(solution)/shard_map/ppermute | solution.py:20
  16.8 6.6 %collective-permute-start.3 = (bf16[4,256,128]{2,1,0:T(8,128)(2,1)S(1)}, bf16[4,256,128]{2,1,0:T(8,128)(2,1)S(1)}, u32[]{:S(2)}, u32[]{:S(2)}) collective-permute-start(bf16[4,256,128]{2,1,0:T(8,128)(2,1)S(1)} %shard_map.68.refs_0_), channel_id=1, source_target_pairs={{0,1},{1,0},{2,3},{3,2},{4,5},{5,4},{6,7},{7,6},{8,9},{9,8},{10,11... | collective-permute-start | bytes 786440 | tf_op jit(solution)/shard_map/ppermute | solution.py:20
  23.4 1.5 collective-permute-start.5
  24.9 1.6 %copy-start.3 = (bf16[4,256,1024]{2,1,0:T(8,128)(2,1)S(1)}, bf16[4,256,1024]{2,1,0:T(8,128)(2,1)}, u32[]{:S(2)}) copy-start(bf16[4,256,1024]{2,1,0:T(8,128)(2,1)} %down_ref.5) | copy-start | bytes 6291460
  26.5 28.1 %copy-start.1 = (bf16[4,256,1024]{2,1,0:T(8,128)(2,1)S(1)}, bf16[4,256,1024]{2,1,0:T(8,128)(2,1)}, u32[]{:S(2)}) copy-start(bf16[4,256,1024]{2,1,0:T(8,128)(2,1)} %blocks_ref.7) | copy-start | bytes 6291460
  29.7 11.1 %collective-permute-start.6 = (bf16[4,256,128]{2,1,0:T(8,128)(2,1)S(1)}, bf16[4,256,128]{2,1,0:T(8,128)(2,1)S(1)}, u32[]{:S(2)}, u32[]{:S(2)}) collective-permute-start(bf16[4,256,128]{2,1,0:T(8,128)(2,1)S(1)} %get-tuple-element.14), channel_id=1, source_target_pairs={{0,4},{4,8},{8,12},{12,0},{1,5},{5,9},{9,13},{13,1},{2,6},{6,10},{... | collective-permute-start | bytes 786440 | tf_op jit(solution)/shard_map/ppermute | solution.py:25
  31.6 13.7 %collective-permute-start.7 = (bf16[4,256,128]{2,1,0:T(8,128)(2,1)S(1)}, bf16[4,256,128]{2,1,0:T(8,128)(2,1)S(1)}, u32[]{:S(2)}, u32[]{:S(2)}) collective-permute-start(bf16[4,256,128]{2,1,0:T(8,128)(2,1)S(1)} %get-tuple-element.15), channel_id=1, source_target_pairs={{0,12},{4,0},{8,4},{12,8},{1,13},{5,1},{9,5},{13,9},{2,14},{6,2},{... | collective-permute-start | bytes 786440 | tf_op jit(solution)/shard_map/ppermute | solution.py:25
  45.4 7.7 %collective-permute-start.9 = (bf16[4,256,128]{2,1,0:T(8,128)(2,1)S(1)}, bf16[4,256,128]{2,1,0:T(8,128)(2,1)S(1)}, u32[]{:S(2)}, u32[]{:S(2)}) collective-permute-start(bf16[4,256,128]{2,1,0:T(8,128)(2,1)S(1)} %fusion.refs_0_), channel_id=1, source_target_pairs={{0,2},{1,3},{2,0},{3,1},{4,6},{5,7},{6,4},{7,5},{8,10},{9,11},{10,... | collective-permute-start | bytes 786440 | tf_op jit(solution)/shard_map/ppermute | solution.py:20
  46.9 6.2 %collective-permute-start.8 = (bf16[4,256,128]{2,1,0:T(8,128)(2,1)S(1)}, bf16[4,256,128]{2,1,0:T(8,128)(2,1)S(1)}, u32[]{:S(2)}, u32[]{:S(2)}) collective-permute-start(bf16[4,256,128]{2,1,0:T(8,128)(2,1)S(1)} %fusion.refs_0_), channel_id=1, source_target_pairs={{0,1},{1,0},{2,3},{3,2},{4,5},{5,4},{6,7},{7,6},{8,9},{9,8},{10,11... | collective-permute-start | bytes 786440 | tf_op jit(solution)/shard_map/ppermute | solution.py:20
  53.1 1.5 collective-permute-start.10
  55.4 8.4 %collective-permute-start.12 = (bf16[4,256,128]{2,1,0:T(8,128)(2,1)S(1)}, bf16[4,256,128]{2,1,0:T(8,128)(2,1)S(1)}, u32[]{:S(2)}, u32[]{:S(2)}) collective-permute-start(bf16[4,256,128]{2,1,0:T(8,128)(2,1)S(1)} %shard_map.70.refs_0_), channel_id=1, source_target_pairs={{0,2},{1,3},{2,0},{3,1},{4,6},{5,7},{6,4},{7,5},{8,10},{9,11},{10,... | collective-permute-start | bytes 786440 | tf_op jit(solution)/shard_map/ppermute | solution.py:20
  56.9 6.9 %collective-permute-start.11 = (bf16[4,256,128]{2,1,0:T(8,128)(2,1)S(1)}, bf16[4,256,128]{2,1,0:T(8,128)(2,1)S(1)}, u32[]{:S(2)}, u32[]{:S(2)}) collective-permute-start(bf16[4,256,128]{2,1,0:T(8,128)(2,1)S(1)} %shard_map.70.refs_0_), channel_id=1, source_target_pairs={{0,1},{1,0},{2,3},{3,2},{4,5},{5,4},{6,7},{7,6},{8,9},{9,8},{10,11... | collective-permute-start | bytes 786440 | tf_op jit(solution)/shard_map/ppermute | solution.py:20
  63.8 1.5 collective-permute-start.13
  68.4 11.1 %collective-permute-start.14 = (bf16[4,256,128]{2,1,0:T(8,128)(2,1)S(1)}, bf16[4,256,128]{2,1,0:T(8,128)(2,1)S(1)}, u32[]{:S(2)}, u32[]{:S(2)}) collective-permute-start(bf16[4,256,128]{2,1,0:T(8,128)(2,1)S(1)} %get-tuple-element.17), channel_id=1, source_target_pairs={{0,4},{4,8},{8,12},{12,0},{1,5},{5,9},{9,13},{13,1},{2,6},{6,10},{... | collective-permute-start | bytes 786440 | tf_op jit(solution)/shard_map/ppermute | solution.py:25
  70.2 13.7 %collective-permute-start.15 = (bf16[4,256,128]{2,1,0:T(8,128)(2,1)S(1)}, bf16[4,256,128]{2,1,0:T(8,128)(2,1)S(1)}, u32[]{:S(2)}, u32[]{:S(2)}) collective-permute-start(bf16[4,256,128]{2,1,0:T(8,128)(2,1)S(1)} %get-tuple-element.18), channel_id=1, source_target_pairs={{0,12},{4,0},{8,4},{12,8},{1,13},{5,1},{9,5},{13,9},{2,14},{6,2},{... | collective-permute-start | bytes 786440 | tf_op jit(solution)/shard_map/ppermute | solution.py:25
  84.0 7.9 %collective-permute-start.17 = (bf16[4,256,128]{2,1,0:T(8,128)(2,1)S(1)}, bf16[4,256,128]{2,1,0:T(8,128)(2,1)S(1)}, u32[]{:S(2)}, u32[]{:S(2)}) collective-permute-start(bf16[4,256,128]{2,1,0:T(8,128)(2,1)S(1)} %fusion.1.refs_0_), channel_id=1, source_target_pairs={{0,2},{1,3},{2,0},{3,1},{4,6},{5,7},{6,4},{7,5},{8,10},{9,11},{10,... | collective-permute-start | bytes 786440 | tf_op jit(solution)/shard_map/ppermute | solution.py:20
  85.5 6.4 %collective-permute-start.16 = (bf16[4,256,128]{2,1,0:T(8,128)(2,1)S(1)}, bf16[4,256,128]{2,1,0:T(8,128)(2,1)S(1)}, u32[]{:S(2)}, u32[]{:S(2)}) collective-permute-start(bf16[4,256,128]{2,1,0:T(8,128)(2,1)S(1)} %fusion.1.refs_0_), channel_id=1, source_target_pairs={{0,1},{1,0},{2,3},{3,2},{4,5},{5,4},{6,7},{7,6},{8,9},{9,8},{10,11... | collective-permute-start | bytes 786440 | tf_op jit(solution)/shard_map/ppermute | solution.py:20
  91.9 1.5 collective-permute-start.18
  94.2 8.4 %collective-permute-start.20 = (bf16[4,256,128]{2,1,0:T(8,128)(2,1)S(1)}, bf16[4,256,128]{2,1,0:T(8,128)(2,1)S(1)}, u32[]{:S(2)}, u32[]{:S(2)}) collective-permute-start(bf16[4,256,128]{2,1,0:T(8,128)(2,1)S(1)} %shard_map.72.refs_0_), channel_id=1, source_target_pairs={{0,2},{1,3},{2,0},{3,1},{4,6},{5,7},{6,4},{7,5},{8,10},{9,11},{10,... | collective-permute-start | bytes 786440 | tf_op jit(solution)/shard_map/ppermute | solution.py:20
  95.7 6.9 %collective-permute-start.19 = (bf16[4,256,128]{2,1,0:T(8,128)(2,1)S(1)}, bf16[4,256,128]{2,1,0:T(8,128)(2,1)S(1)}, u32[]{:S(2)}, u32[]{:S(2)}) collective-permute-start(bf16[4,256,128]{2,1,0:T(8,128)(2,1)S(1)} %shard_map.72.refs_0_), channel_id=1, source_target_pairs={{0,1},{1,0},{2,3},{3,2},{4,5},{5,4},{6,7},{7,6},{8,9},{9,8},{10,11... | collective-permute-start | bytes 786440 | tf_op jit(solution)/shard_map/ppermute | solution.py:20
  102.6 1.5 collective-permute-start.21
  107.2 11.1 %collective-permute-start.22 = (bf16[4,256,128]{2,1,0:T(8,128)(2,1)S(1)}, bf16[4,256,128]{2,1,0:T(8,128)(2,1)S(1)}, u32[]{:S(2)}, u32[]{:S(2)}) collective-permute-start(bf16[4,256,128]{2,1,0:T(8,128)(2,1)S(1)} %get-tuple-element.20), channel_id=1, source_target_pairs={{0,4},{4,8},{8,12},{12,0},{1,5},{5,9},{9,13},{13,1},{2,6},{6,10},{... | collective-permute-start | bytes 786440 | tf_op jit(solution)/shard_map/ppermute | solution.py:25
  107.4 14.1 %collective-permute-start.23 = (bf16[4,256,128]{2,1,0:T(8,128)(2,1)S(1)}, bf16[4,256,128]{2,1,0:T(8,128)(2,1)S(1)}, u32[]{:S(2)}, u32[]{:S(2)}) collective-permute-start(bf16[4,256,128]{2,1,0:T(8,128)(2,1)S(1)} %get-tuple-element.21), channel_id=1, source_target_pairs={{0,12},{4,0},{8,4},{12,8},{1,13},{5,1},{9,5},{13,9},{2,14},{6,2},{... | collective-permute-start | bytes 786440 | tf_op jit(solution)/shard_map/ppermute | solution.py:25
  121.7 7.6 %collective-permute-start.25 = (bf16[4,256,128]{2,1,0:T(8,128)(2,1)S(1)}, bf16[4,256,128]{2,1,0:T(8,128)(2,1)S(1)}, u32[]{:S(2)}, u32[]{:S(2)}) collective-permute-start(bf16[4,256,128]{2,1,0:T(8,128)(2,1)S(1)} %fusion.2.refs_0_), channel_id=1, source_target_pairs={{0,2},{1,3},{2,0},{3,1},{4,6},{5,7},{6,4},{7,5},{8,10},{9,11},{10,... | collective-permute-start | bytes 786440 | tf_op jit(solution)/shard_map/ppermute | solution.py:20
  123.1 6.1 %collective-permute-start.24 = (bf16[4,256,128]{2,1,0:T(8,128)(2,1)S(1)}, bf16[4,256,128]{2,1,0:T(8,128)(2,1)S(1)}, u32[]{:S(2)}, u32[]{:S(2)}) collective-permute-start(bf16[4,256,128]{2,1,0:T(8,128)(2,1)S(1)} %fusion.2.refs_0_), channel_id=1, source_target_pairs={{0,1},{1,0},{2,3},{3,2},{4,5},{5,4},{6,7},{7,6},{8,9},{9,8},{10,11... | collective-permute-start | bytes 786440 | tf_op jit(solution)/shard_map/ppermute | solution.py:20
  129.2 1.5 collective-permute-start.26
  132.4 1.3 collective-permute-start.27
  133.8 4.3 %collective-permute-start.28 = (f32[128,128]{1,0:T(8,128)S(1)}, f32[128,128]{1,0:T(8,128)S(1)}, u32[]{:S(2)}, u32[]{:S(2)}) collective-permute-start(f32[128,128]{1,0:T(8,128)S(1)} %add.36), channel_id=1, source_target_pairs={{0,2},{1,3},{2,0},{3,1},{4,6},{5,7},{6,4},{7,5},{8,10},{9,11},{10,... | collective-permute-start | bytes 196616 | tf_op jit(solution)/shard_map/ppermute | solution.py:20
  138.1 4.3 %collective-permute-start.29 = (f32[128,128]{1,0:T(8,128)S(1)}, f32[128,128]{1,0:T(8,128)S(1)}, u32[]{:S(2)}, u32[]{:S(2)}) collective-permute-start(f32[128,128]{1,0:T(8,128)S(1)} %add.37), channel_id=1, source_target_pairs={{0,4},{4,0},{8,12},{12,8},{1,5},{5,1},{9,13},{13,9},{2,6},{6,2},{1... | collective-permute-start | bytes 196616 | tf_op jit(solution)/shard_map/ppermute | solution.py:20
  142.4 5.8 %collective-permute-start.30 = (f32[128,128]{1,0:T(8,128)S(1)}, f32[128,128]{1,0:T(8,128)S(1)}, u32[]{:S(2)}, u32[]{:S(2)}) collective-permute-start(f32[128,128]{1,0:T(8,128)S(1)} %add.38), channel_id=1, source_target_pairs={{0,8},{4,12},{8,0},{12,4},{1,9},{5,13},{9,1},{13,5},{2,10},{6,14},... | collective-permute-start | bytes 196616 | tf_op jit(solution)/shard_map/ppermute | solution.py:20

commit v3 on v2

v3 whole, which is shorter than its diff:
```python
import functools

import jax
import jax.numpy as jnp
from jax import lax
from jax.experimental import pallas as pl
from jax.experimental.pallas import tpu as pltpu
from jax.sharding import PartitionSpec as P

BAND = 4
SWEEPS = 3
CHUNKS = 2
SUB = 8
F32 = jnp.float32
BF16 = jnp.bfloat16
VMEM = pl.BlockSpec(memory_space=pltpu.VMEM)
SMEM = pl.BlockSpec(memory_space=pltpu.SMEM)


def flip(value, axis, mask):
    return lax.ppermute(value, axis, [(i, i ^ mask) for i in range(lax.axis_size(axis))])


def turn(value, axis, step):
    count = lax.axis_size(axis)
    return lax.ppermute(value, axis, [(i, (i + step) % count) for i in range(count)])


def wall_pieces(own):
    pieces = {0: own}
    bit = lax.axis_size("wall") // 2
    while bit:
        for mask in list(pieces):
            pieces[mask ^ bit] = flip(pieces[mask], "wall", bit)
        bit //= 2
    return [pieces[mask] for mask in range(len(pieces))]


def params(mib):
    return pltpu.CompilerParams(vmem_limit_bytes=mib << 20)


def cost(flops, *arrays):
    moved = sum(a.size * a.dtype.itemsize for a in arrays)
    return pl.CostEstimate(flops=flops, bytes_accessed=moved, transcendentals=0)


def turned_dot(left, right, **how):
    return lax.dot_general(left, right, (((1,), (1,)), ((), ())), preferred_element_type=F32, **how)


def ordered(weights_ref, index, place, shards):
    rows = weights_ref.shape[2] // shards
    return jnp.concatenate(
        [
            weights_ref[index, :, pl.ds(pl.multiple_of((place ^ mask) * rows, rows), rows)]
            for mask in range(shards)
        ],
        axis=1,
    )


def split_kernel(sketch_ref, *chunk_refs):
    part = chunk_refs[0].shape[1]
    for h in range(sketch_ref.shape[0]):
        turned = sketch_ref[h].T
        for i, ref in enumerate(chunk_refs):
            ref[h] = turned[i * part : (i + 1) * part]


def split(sketch):
    count, rows, width = sketch.shape
    out = jax.ShapeDtypeStruct((count, width // CHUNKS, rows), BF16)
    return pl.pallas_call(
        split_kernel,
        out_shape=[out] * CHUNKS,
        in_specs=[VMEM],
        out_specs=[VMEM] * CHUNKS,
        compiler_params=params(4),
        cost_estimate=cost(0, sketch, sketch),
    )(sketch)


def inverse_kernel(shards, place_ref, blocks_ref, *refs):
    pieces, out_ref = refs[:shards], refs[shards]
    for h in range(out_ref.shape[0]):
        wide = jnp.concatenate([p[h] for p in pieces], axis=1)
        total = turned_dot(wide, ordered(blocks_ref, h, place_ref[0], shards))
        out_ref[h] = total.astype(out_ref.dtype)


def apply_inverse(place, blocks, source, dtype):
    pieces = wall_pieces(source)
    return pl.pallas_call(
        functools.partial(inverse_kernel, len(pieces)),
        out_shape=jax.ShapeDtypeStruct(source.shape, dtype),
        in_specs=[SMEM, VMEM] + [VMEM] * len(pieces),
        out_specs=VMEM,
        compiler_params=params(12),
        cost_estimate=cost(2 * blocks.size * source.shape[1], blocks, *pieces),
    )(place, blocks, *pieces)


def couple_kernel(shards, place_ref, strip_ref, up_ref, down_ref, *refs):
    pieces = refs[:shards]
    own_ref, below_ref, above_ref, total = refs[shards:]
    count, part, rows = pieces[0].shape
    total[...] = jnp.zeros_like(total)
    wide = jnp.concatenate([p[...].reshape(count * part, rows) for p in pieces], axis=1)
    for j in range(BAND):
        offset = strip_ref[j] + 1
        for weights, shift in ((up_ref, offset), (down_ref, -offset)):
            added = turned_dot(wide, ordered(weights, j, place_ref[0], shards))
            total[pl.ds(BAND + shift, count)] += added.reshape(count, part, rows)
    own_ref[...] = total[BAND : BAND + count]
    below_ref[...] = total[:BAND].astype(below_ref.dtype)
    above_ref[...] = total[BAND + count :].astype(above_ref.dtype)


def couple(place, strips, up, down, state):
    pieces = wall_pieces(state)
    count, part, rows = state.shape
    halo = jax.ShapeDtypeStruct((BAND, part, rows), BF16)
    own, below, above = pl.pallas_call(
        functools.partial(couple_kernel, len(pieces)),
        out_shape=[jax.ShapeDtypeStruct(state.shape, F32), halo, halo],
        in_specs=[SMEM, SMEM, VMEM, VMEM] + [VMEM] * len(pieces),
        out_specs=[VMEM] * 3,
        scratch_shapes=[pltpu.VMEM((count + 2 * BAND, part, rows), F32)],
        compiler_params=params(20),
        cost_estimate=cost(2 * (up.size + down.size) * count * part, up, down, *pieces),
    )(place, strips, up, down, *pieces)
    before = turn(above, "harm", 1).astype(F32)
    after = turn(below, "harm", -1).astype(F32)
    if count == BAND:
        return own + before + after
    return own.at[:BAND].add(before).at[count - BAND :].add(after)


def all_sum(value):
    for axis in ("wall", "harm"):
        bit = 1
        while bit < lax.axis_size(axis):
            value = value + flip(value, axis, bit)
            bit *= 2
    return value


def gram_kernel(*refs):
    chunks, gram_ref = refs[:-1], refs[-1]
    gram = jnp.zeros(gram_ref.shape, F32)
    for h in range(chunks[0].shape[0]):
        wide = jnp.concatenate([c[h] for c in chunks], axis=0)
        gram += turned_dot(wide, wide, precision=lax.Precision.HIGHEST)
    gram_ref[...] = gram


def gram_of(chunks):
    width = sum(c.shape[1] for c in chunks)
    return pl.pallas_call(
        gram_kernel,
        out_shape=jax.ShapeDtypeStruct((width, width), F32),
        in_specs=[VMEM] * len(chunks),
        out_specs=VMEM,
        compiler_params=params(8),
    )(*chunks)


def spread(row, height):
    return jnp.broadcast_to(row, (height, row.shape[1]))


def factor(gram):
    size = gram.shape[0]
    panels = size // SUB
    level = lax.broadcasted_iota(jnp.int32, (SUB, size), 0)
    lane = lax.broadcasted_iota(jnp.int32, (SUB, size), 1)
    upper = [gram[SUB * p : SUB * (p + 1)] for p in range(panels)]
    inverse = [jnp.where(lane == level + SUB * p, 1.0, 0.0) for p in range(panels)]
    for p in range(panels):
        column = {
            q: [
                jnp.broadcast_to(upper[q][:, SUB * p + j : SUB * p + j + 1], (SUB, size))
                for j in range(SUB)
            ]
            for q in range(p, panels)
        }
        for k in range(SUB):
            scale = lax.rsqrt(spread(column[p][k][k : k + 1], SUB))
            heads = [spread(column[p][j][k : k + 1], SUB) * scale for j in range(k + 1, SUB)]
            row = spread(upper[p][k : k + 1], SUB) * scale
            back = spread(inverse[p][k : k + 1], SUB) * scale
            for q in range(p, panels):
                part = column[q][k] * scale
                if q == p:
                    part = jnp.where(level > k, part, 0.0)
                for j, head in enumerate(heads):
                    column[q][k + 1 + j] -= part * head
                upper[q] -= part * row
                inverse[q] -= part * back
            upper[p] = jnp.where(level == k, row, upper[p])
            inverse[p] = jnp.where(level == k, back, inverse[p])
    for p in range(panels):
        upper[p] = jnp.where(lane >= level + SUB * p, upper[p], 0.0)
        inverse[p] = jnp.where(lane <= level + SUB * p, inverse[p], 0.0)
    return upper, inverse


def basis_kernel(entries, gram_ref, *refs):
    chunks = refs[:CHUNKS]
    basis_ref, triangle_ref, inverse_ref = refs[CHUNKS:]
    upper, inverse = factor(gram_ref[...] / entries)
    for p, rows in enumerate(upper):
        triangle_ref[SUB * p : SUB * (p + 1)] = rows
    for p, rows in enumerate(inverse):
        inverse_ref[SUB * p : SUB * (p + 1)] = rows
    for h in range(basis_ref.shape[0]):
        wide = jnp.concatenate([c[h] for c in chunks], axis=0)
        basis_ref[h] = jnp.dot(
            inverse_ref[...],
            wide,
            precision=lax.Precision.HIGHEST,
            preferred_element_type=F32,
        ).T


def basis_of(gram, chunks, shape, entries):
    return pl.pallas_call(
        functools.partial(basis_kernel, entries),
        out_shape=[jax.ShapeDtypeStruct(shape, F32), jax.ShapeDtypeStruct(gram.shape, F32)],
        in_specs=[VMEM] * (1 + CHUNKS),
        out_specs=[VMEM, VMEM],
        scratch_shapes=[pltpu.VMEM(gram.shape, F32)],
        compiler_params=params(12),
    )(gram, *chunks)


def body(sketch, inverse_blocks, couple_up, couple_down, strip_harmonics):
    count, rows, width = sketch.shape
    place = lax.axis_index("wall").astype(jnp.int32).reshape(1)
    sampled = []
    for chunk in split(sketch):
        state = apply_inverse(place, inverse_blocks, chunk, BF16)
        for sweep in range(SWEEPS):
            coupled = couple(place, strip_harmonics, couple_up, couple_down, state)
            rhs = (chunk.astype(F32) - coupled).astype(BF16)
            last = sweep == SWEEPS - 1
            state = apply_inverse(place, inverse_blocks, rhs, F32 if last else BF16)
        sampled.append(state)
    entries = lax.axis_size("harm") * lax.axis_size("wall") * count * rows
    gram = all_sum(gram_of(sampled))
    return tuple(basis_of(gram, sampled, sketch.shape, entries))


def solution(mesh):
    return jax.shard_map(
        body,
        mesh=mesh,
        in_specs=(
            P(("freq", "harm"), "wall", None),
            P(("freq", "harm"), "wall", None),
            P("freq", "wall", None),
            P("freq", "wall", None),
            P("freq"),
        ),
        out_specs=(P(("freq", "harm"), "wall", None), P("freq", None)),
        check_vma=False,
    )
```

time: 154 us -> 133 us (0.86)
  waiting for transfers between devices: 101 us -> 52.5 us
  starting transfers between devices: 28.8 us -> 51.6 us
  Pallas kernels: 18.7 us -> 24.4 us
  local copies, waits for them, and re-layouts: 4.15 us -> 2.54 us
    ppermute x25 -> x46, waiting for transfers between devices: 67.4 us -> 40.8 us  [flip(): lax.ppermute(value, axis, [(i, i ^ mask) for i in range(lax.axis_size(axi...]
    ppermute x6 -> x12, waiting for transfers between devices: 33.6 us -> 11.8 us  [turn(): lax.ppermute(value, axis, [(i, (i + step) % count) for i in range(count)])]
    ppermute x6 -> x12, starting transfers between devices: 11.7 us -> 23.3 us  [turn(): lax.ppermute(value, axis, [(i, (i + step) % count) for i in range(count)])]
    ppermute x25 -> x46, starting transfers between devices: 17.1 us -> 28.3 us  [flip(): lax.ppermute(value, axis, [(i, i ^ mask) for i in range(lax.axis_size(axi...]
    pallas_call x4 -> x10, Pallas kernels: 3.76 us -> 6.85 us  [the longest x8 6.14 us: apply_inverse(): pl.pallas_call(functools.partial(inverse_kernel, len(pieces)), out_shape=...]
    pallas_call x3 -> x6, Pallas kernels: 9.4 us -> 11.9 us  [couple(): pl.pallas_call(functools.partial(couple_kernel, len(pieces)), out_shape=[...]
    unnamed x14 -> x12, local copies, waits for them, and re-layouts: 4.15 us -> 2.54 us
  transfers between devices with their start and end apart: 31 -> 58, of which waited for: 24 -> 24; matrix products, arithmetic and copies ran while one was open for 0% -> 0% of each run, Pallas kernels for 0% -> 13%
where the time goes in v3:
time: 133 us; the launch traced here: 132 us
  waiting for transfers between devices  52.5 us (39%)
  starting transfers between devices  51.6 us (39%)
  Pallas kernels  24.4 us (18%)
  local copies, waits for them, and re-layouts  2.54 us (2%)
    ppermute x46, waiting for transfers between devices, flip(): lax.ppermute(value, axis, [(i, i ^ mask) for i in range(lax.axis_size(axi...  40.8 us
    ppermute x46, starting transfers between devices, flip(): lax.ppermute(value, axis, [(i, i ^ mask) for i in range(lax.axis_size(axi...  28.3 us
    ppermute x12, starting transfers between devices, turn(): lax.ppermute(value, axis, [(i, (i + step) % count) for i in range(count)])  23.3 us
    pallas_call x6, Pallas kernels, couple(): pl.pallas_call(functools.partial(couple_kernel, len(pieces)), out_shape=[...  11.9 us
    ppermute x12, waiting for transfers between devices, turn(): lax.ppermute(value, axis, [(i, (i + step) % count) for i in range(count)])  11.8 us
    pallas_call x8, Pallas kernels, apply_inverse(): pl.pallas_call(functools.partial(inverse_kernel, len(pieces)), out_shape=...  6.14 us
    pallas_call x1, Pallas kernels, basis_of(): pl.pallas_call(functools.partial(basis_kernel, entries), out_shape=[jax.S...  5.58 us
  transfers between devices with their start and end apart: 58, of which 24 were waited for; matrix products, arithmetic and copies ran while one was open for 0% of the time, Pallas kernels for 13%

profile of v3, /device:TPU:0, one launch (start us, length us, event | category | flops | bytes accessed | tf_op | source)
XLA Modules:
  0.0 132.4 jit_solution(5152240498959922044)
XLA Ops:
  1.7 3.0 %collective-permute-start.1 = (bf16[4,64,256]{2,1,0:T(8,128)(2,1)S(1)}, bf16[4,64,256]{2,1,0:T(8,128)(2,1)S(1)}, u32[]{:S(2)}, u32[]{:S(2)}) collective-permute-start(bf16[4,64,256]{2,1,0:T(8,128)(2,1)S(1)} %get-tuple-element.22.refs_0_), channel_id=1, source_target_pairs={{0,2},{1,3},{2,0},{3,1},{4,6},{5,7},{6,4},{7,5},{8,10},{9,11},{10,... | collective-permute-start | bytes 393224 | tf_op jit(solution)/shard_map/ppermute | solution.py:21
  4.8 4.3 %collective-permute-done.1.refs_2_ = bf16[4,64,256]{2,1,0:T(8,128)(2,1)S(1)} collective-permute-done((bf16[4,64,256]{2,1,0:T(8,128)(2,1)S(1)}, bf16[4,64,256]{2,1,0:T(8,128)(2,1)S(1)}, u32[]{:S(2)}, u32[]{:S(2)}) %collective-permute-start.1) | collective-permute-done | bytes 131104 | tf_op jit(solution)/shard_map/ppermute | solution.py:21
  9.6 1.4 %collective-permute-done.28.refs_2_ = bf16[4,64,256]{2,1,0:T(8,128)(2,1)S(1)} collective-permute-done((bf16[4,64,256]{2,1,0:T(8,128)(2,1)S(1)}, bf16[4,64,256]{2,1,0:T(8,128)(2,1)S(1)}, u32[]{:S(2)}, u32[]{:S(2)}) %collective-permute-start.28) | collective-permute-done | bytes 131104 | tf_op jit(solution)/shard_map/ppermute | solution.py:21
  11.1 1.6 %copy-done = bf16[4,256,1024]{2,1,0:T(8,128)(2,1)S(1)} copy-done((bf16[4,256,1024]{2,1,0:T(8,128)(2,1)S(1)}, bf16[4,256,1024]{2,1,0:T(8,128)(2,1)}, u32[]{:S(2)}) %copy-start) | copy-done | bytes 2097176
  13.4 1.8 %collective-permute-start.4 = (bf16[4,64,256]{2,1,0:T(8,128)(2,1)S(1)}, bf16[4,64,256]{2,1,0:T(8,128)(2,1)S(1)}, u32[]{:S(2)}, u32[]{:S(2)}) collective-permute-start(bf16[4,64,256]{2,1,0:T(8,128)(2,1)S(1)} %shard_map.69.refs_0_), channel_id=1, source_target_pairs={{0,2},{1,3},{2,0},{3,1},{4,6},{5,7},{6,4},{7,5},{8,10},{9,11},{10,... | collective-permute-start | bytes 393224 | tf_op jit(solution)/shard_map/ppermute | solution.py:21
  16.4 3.5 %collective-permute-done.4.refs_2_ = bf16[4,64,256]{2,1,0:T(8,128)(2,1)S(1)} collective-permute-done((bf16[4,64,256]{2,1,0:T(8,128)(2,1)S(1)}, bf16[4,64,256]{2,1,0:T(8,128)(2,1)S(1)}, u32[]{:S(2)}, u32[]{:S(2)}) %collective-permute-start.4) | collective-permute-done | bytes 131104 | tf_op jit(solution)/shard_map/ppermute | solution.py:21
  20.4 1.8 %collective-permute-done.31.refs_2_ = bf16[4,64,256]{2,1,0:T(8,128)(2,1)S(1)} collective-permute-done((bf16[4,64,256]{2,1,0:T(8,128)(2,1)S(1)}, bf16[4,64,256]{2,1,0:T(8,128)(2,1)S(1)}, u32[]{:S(2)}, u32[]{:S(2)}) %collective-permute-start.31) | collective-permute-done | bytes 131104 | tf_op jit(solution)/shard_map/ppermute | solution.py:21
  22.2 2.0 %shard_map.70 = (f32[4,64,256]{2,1,0:T(8,128)S(1)}, bf16[4,64,256]{2,1,0:T(8,128)(2,1)S(1)}, bf16[4,64,256]{2,1,0:T(8,128)(2,1)S(1)}) custom-call(s32[1]{0:T(128)} %bitcast.place_ref, s32[4]{0:T(128)S(1)} %copy-done.5, bf16[4,256,1024]{2,1,0:T(8,128)(2,1)S(1)} %copy-done.2, bf16[4,256,1024]{2,1,0:T(8,128)(2,1)S(1)} %copy-done.3, ...), custom_call_target="tpu_custom_call" | custom-call | flops 1073741824 | bytes 4718592 | tf_op jit(solution)/shard_map/pallas_call | solution.py:124
  24.3 1.9 %collective-permute-start.6 = (bf16[4,64,256]{2,1,0:T(8,128)(2,1)S(1)}, bf16[4,64,256]{2,1,0:T(8,128)(2,1)S(1)}, u32[]{:S(2)}, u32[]{:S(2)}) collective-permute-start(bf16[4,64,256]{2,1,0:T(8,128)(2,1)S(1)} %get-tuple-element.24), channel_id=1, source_target_pairs={{0,4},{4,8},{8,12},{12,0},{1,5},{5,9},{9,13},{13,1},{2,6},{6,10},{... | collective-permute-start | bytes 393224 | tf_op jit(solution)/shard_map/ppermute | solution.py:26
  26.1 2.1 %collective-permute-start.7 = (bf16[4,64,256]{2,1,0:T(8,128)(2,1)S(1)}, bf16[4,64,256]{2,1,0:T(8,128)(2,1)S(1)}, u32[]{:S(2)}, u32[]{:S(2)}) collective-permute-start(bf16[4,64,256]{2,1,0:T(8,128)(2,1)S(1)} %get-tuple-element.25), channel_id=1, source_target_pairs={{0,12},{4,0},{8,4},{12,8},{1,13},{5,1},{9,5},{13,9},{2,14},{6,2},{... | collective-permute-start | bytes 393224 | tf_op jit(solution)/shard_map/ppermute | solution.py:26
  28.2 2.0 %shard_map.77 = (f32[4,64,256]{2,1,0:T(8,128)S(1)}, bf16[4,64,256]{2,1,0:T(8,128)(2,1)S(1)}, bf16[4,64,256]{2,1,0:T(8,128)(2,1)S(1)}) custom-call(s32[1]{0:T(128)} %bitcast.place_ref, s32[4]{0:T(128)S(1)} %copy-done.5, bf16[4,256,1024]{2,1,0:T(8,128)(2,1)S(1)} %copy-done.2, bf16[4,256,1024]{2,1,0:T(8,128)(2,1)S(1)} %copy-done.3, ...), custom_call_target="tpu_custom_call" | custom-call | flops 1073741824 | bytes 4718592 | tf_op jit(solution)/shard_map/pallas_call | solution.py:124
  30.3 3.8 %collective-permute-start.34 = (bf16[4,64,256]{2,1,0:T(8,128)(2,1)S(1)}, bf16[4,64,256]{2,1,0:T(8,128)(2,1)S(1)}, u32[]{:S(2)}, u32[]{:S(2)}) collective-permute-start(bf16[4,64,256]{2,1,0:T(8,128)(2,1)S(1)} %get-tuple-element.35), channel_id=1, source_target_pairs={{0,12},{4,0},{8,4},{12,8},{1,13},{5,1},{9,5},{13,9},{2,14},{6,2},{... | collective-permute-start | bytes 393224 | tf_op jit(solution)/shard_map/ppermute | solution.py:26
  35.5 1.6 %collective-permute-start.9 = (bf16[4,64,256]{2,1,0:T(8,128)(2,1)S(1)}, bf16[4,64,256]{2,1,0:T(8,128)(2,1)S(1)}, u32[]{:S(2)}, u32[]{:S(2)}) collective-permute-start(bf16[4,64,256]{2,1,0:T(8,128)(2,1)S(1)} %fusion.refs_0_), channel_id=1, source_target_pairs={{0,2},{1,3},{2,0},{3,1},{4,6},{5,7},{6,4},{7,5},{8,10},{9,11},{10,... | collective-permute-start | bytes 393224 | tf_op jit(solution)/shard_map/ppermute | solution.py:21
  37.1 1.4 %collective-permute-done.33 = bf16[4,64,256]{2,1,0:T(8,128)(2,1)S(1)} collective-permute-done((bf16[4,64,256]{2,1,0:T(8,128)(2,1)S(1)}, bf16[4,64,256]{2,1,0:T(8,128)(2,1)S(1)}, u32[]{:S(2)}, u32[]{:S(2)}) %collective-permute-start.33) | collective-permute-done | bytes 131104 | tf_op jit(solution)/shard_map/ppermute | solution.py:26
  38.5 1.7 %collective-permute-done.34 = bf16[4,64,256]{2,1,0:T(8,128)(2,1)S(1)} collective-permute-done((bf16[4,64,256]{2,1,0:T(8,128)(2,1)S(1)}, bf16[4,64,256]{2,1,0:T(8,128)(2,1)S(1)}, u32[]{:S(2)}, u32[]{:S(2)}) %collective-permute-start.34) | collective-permute-done | bytes 131104 | tf_op jit(solution)/shard_map/ppermute | solution.py:26
  40.3 1.6 %collective-permute-start.36 = (bf16[4,64,256]{2,1,0:T(8,128)(2,1)S(1)}, bf16[4,64,256]{2,1,0:T(8,128)(2,1)S(1)}, u32[]{:S(2)}, u32[]{:S(2)}) collective-permute-start(bf16[4,64,256]{2,1,0:T(8,128)(2,1)S(1)} %fusion.3.refs_0_), channel_id=1, source_target_pairs={{0,2},{1,3},{2,0},{3,1},{4,6},{5,7},{6,4},{7,5},{8,10},{9,11},{10,... | collective-permute-start | bytes 393224 | tf_op jit(solution)/shard_map/ppermute | solution.py:21
  42.3 3.0 %collective-permute-done.36.refs_2_ = bf16[4,64,256]{2,1,0:T(8,128)(2,1)S(1)} collective-permute-done((bf16[4,64,256]{2,1,0:T(8,128)(2,1)S(1)}, bf16[4,64,256]{2,1,0:T(8,128)(2,1)S(1)}, u32[]{:S(2)}, u32[]{:S(2)}) %collective-permute-start.36) | collective-permute-done | bytes 131104 | tf_op jit(solution)/shard_map/ppermute | solution.py:21
  46.1 1.6 %collective-permute-start.12 = (bf16[4,64,256]{2,1,0:T(8,128)(2,1)S(1)}, bf16[4,64,256]{2,1,0:T(8,128)(2,1)S(1)}, u32[]{:S(2)}, u32[]{:S(2)}) collective-permute-start(bf16[4,64,256]{2,1,0:T(8,128)(2,1)S(1)} %shard_map.71.refs_0_), channel_id=1, source_target_pairs={{0,2},{1,3},{2,0},{3,1},{4,6},{5,7},{6,4},{7,5},{8,10},{9,11},{10,... | collective-permute-start | bytes 393224 | tf_op jit(solution)/shard_map/ppermute | solution.py:21
  49.0 3.5 %collective-permute-done.12.refs_2_ = bf16[4,64,256]{2,1,0:T(8,128)(2,1)S(1)} collective-permute-done((bf16[4,64,256]{2,1,0:T(8,128)(2,1)S(1)}, bf16[4,64,256]{2,1,0:T(8,128)(2,1)S(1)}, u32[]{:S(2)}, u32[]{:S(2)}) %collective-permute-start.12) | collective-permute-done | bytes 131104 | tf_op jit(solution)/shard_map/ppermute | solution.py:21
  53.0 1.8 %collective-permute-done.39.refs_2_ = bf16[4,64,256]{2,1,0:T(8,128)(2,1)S(1)} collective-permute-done((bf16[4,64,256]{2,1,0:T(8,128)(2,1)S(1)}, bf16[4,64,256]{2,1,0:T(8,128)(2,1)S(1)}, u32[]{:S(2)}, u32[]{:S(2)}) %collective-permute-start.39) | collective-permute-done | bytes 131104 | tf_op jit(solution)/shard_map/ppermute | solution.py:21
  54.9 2.0 %shard_map.72 = (f32[4,64,256]{2,1,0:T(8,128)S(1)}, bf16[4,64,256]{2,1,0:T(8,128)(2,1)S(1)}, bf16[4,64,256]{2,1,0:T(8,128)(2,1)S(1)}) custom-call(s32[1]{0:T(128)} %bitcast.place_ref, s32[4]{0:T(128)S(1)} %copy-done.5, bf16[4,256,1024]{2,1,0:T(8,128)(2,1)S(1)} %copy-done.2, bf16[4,256,1024]{2,1,0:T(8,128)(2,1)S(1)} %copy-done.3, ...), custom_call_target="tpu_custom_call" | custom-call | flops 1073741824 | bytes 4718592 | tf_op jit(solution)/shard_map/pallas_call | solution.py:124
  56.9 1.7 %collective-permute-start.14 = (bf16[4,64,256]{2,1,0:T(8,128)(2,1)S(1)}, bf16[4,64,256]{2,1,0:T(8,128)(2,1)S(1)}, u32[]{:S(2)}, u32[]{:S(2)}) collective-permute-start(bf16[4,64,256]{2,1,0:T(8,128)(2,1)S(1)} %get-tuple-element.27), channel_id=1, source_target_pairs={{0,4},{4,8},{8,12},{12,0},{1,5},{5,9},{9,13},{13,1},{2,6},{6,10},{... | collective-permute-start | bytes 393224 | tf_op jit(solution)/shard_map/ppermute | solution.py:26
  58.5 2.2 %collective-permute-start.15 = (bf16[4,64,256]{2,1,0:T(8,128)(2,1)S(1)}, bf16[4,64,256]{2,1,0:T(8,128)(2,1)S(1)}, u32[]{:S(2)}, u32[]{:S(2)}) collective-permute-start(bf16[4,64,256]{2,1,0:T(8,128)(2,1)S(1)} %get-tuple-element.28), channel_id=1, source_target_pairs={{0,12},{4,0},{8,4},{12,8},{1,13},{5,1},{9,5},{13,9},{2,14},{6,2},{... | collective-permute-start | bytes 393224 | tf_op jit(solution)/shard_map/ppermute | solution.py:26
  60.8 2.0 %shard_map.79 = (f32[4,64,256]{2,1,0:T(8,128)S(1)}, bf16[4,64,256]{2,1,0:T(8,128)(2,1)S(1)}, bf16[4,64,256]{2,1,0:T(8,128)(2,1)S(1)}) custom-call(s32[1]{0:T(128)} %bitcast.place_ref, s32[4]{0:T(128)S(1)} %copy-done.5, bf16[4,256,1024]{2,1,0:T(8,128)(2,1)S(1)} %copy-done.2, bf16[4,256,1024]{2,1,0:T(8,128)(2,1)S(1)} %copy-done.3, ...), custom_call_target="tpu_custom_call" | custom-call | flops 1073741824 | bytes 4718592 | tf_op jit(solution)/shard_map/pallas_call | solution.py:124
  62.8 3.8 %collective-permute-start.42 = (bf16[4,64,256]{2,1,0:T(8,128)(2,1)S(1)}, bf16[4,64,256]{2,1,0:T(8,128)(2,1)S(1)}, u32[]{:S(2)}, u32[]{:S(2)}) collective-permute-start(bf16[4,64,256]{2,1,0:T(8,128)(2,1)S(1)} %get-tuple-element.38), channel_id=1, source_target_pairs={{0,12},{4,0},{8,4},{12,8},{1,13},{5,1},{9,5},{13,9},{2,14},{6,2},{... | collective-permute-start | bytes 393224 | tf_op jit(solution)/shard_map/ppermute | solution.py:26
  68.0 1.5 %collective-permute-start.17 = (bf16[4,64,256]{2,1,0:T(8,128)(2,1)S(1)}, bf16[4,64,256]{2,1,0:T(8,128)(2,1)S(1)}, u32[]{:S(2)}, u32[]{:S(2)}) collective-permute-start(bf16[4,64,256]{2,1,0:T(8,128)(2,1)S(1)} %fusion.1.refs_0_), channel_id=1, source_target_pairs={{0,2},{1,3},{2,0},{3,1},{4,6},{5,7},{6,4},{7,5},{8,10},{9,11},{10,... | collective-permute-start | bytes 393224 | tf_op jit(solution)/shard_map/ppermute | solution.py:21
  69.5 1.5 %collective-permute-done.41 = bf16[4,64,256]{2,1,0:T(8,128)(2,1)S(1)} collective-permute-done((bf16[4,64,256]{2,1,0:T(8,128)(2,1)S(1)}, bf16[4,64,256]{2,1,0:T(8,128)(2,1)S(1)}, u32[]{:S(2)}, u32[]{:S(2)}) %collective-permute-start.41) | collective-permute-done | bytes 131104 | tf_op jit(solution)/shard_map/ppermute | solution.py:26
  71.0 1.6 %collective-permute-done.42 = bf16[4,64,256]{2,1,0:T(8,128)(2,1)S(1)} collective-permute-done((bf16[4,64,256]{2,1,0:T(8,128)(2,1)S(1)}, bf16[4,64,256]{2,1,0:T(8,128)(2,1)S(1)}, u32[]{:S(2)}, u32[]{:S(2)}) %collective-permute-start.42) | collective-permute-done | bytes 131104 | tf_op jit(solution)/shard_map/ppermute | solution.py:26
  72.7 1.6 %collective-permute-start.44 = (bf16[4,64,256]{2,1,0:T(8,128)(2,1)S(1)}, bf16[4,64,256]{2,1,0:T(8,128)(2,1)S(1)}, u32[]{:S(2)}, u32[]{:S(2)}) collective-permute-start(bf16[4,64,256]{2,1,0:T(8,128)(2,1)S(1)} %fusion.4.refs_0_), channel_id=1, source_target_pairs={{0,2},{1,3},{2,0},{3,1},{4,6},{5,7},{6,4},{7,5},{8,10},{9,11},{10,... | collective-permute-start | bytes 393224 | tf_op jit(solution)/shard_map/ppermute | solution.py:21
  74.7 3.0 %collective-permute-done.44.refs_2_ = bf16[4,64,256]{2,1,0:T(8,128)(2,1)S(1)} collective-permute-done((bf16[4,64,256]{2,1,0:T(8,128)(2,1)S(1)}, bf16[4,64,256]{2,1,0:T(8,128)(2,1)S(1)}, u32[]{:S(2)}, u32[]{:S(2)}) %collective-permute-start.44) | collective-permute-done | bytes 131104 | tf_op jit(solution)/shard_map/ppermute | solution.py:21
  78.5 1.6 %collective-permute-start.20 = (bf16[4,64,256]{2,1,0:T(8,128)(2,1)S(1)}, bf16[4,64,256]{2,1,0:T(8,128)(2,1)S(1)}, u32[]{:S(2)}, u32[]{:S(2)}) collective-permute-start(bf16[4,64,256]{2,1,0:T(8,128)(2,1)S(1)} %shard_map.73.refs_0_), channel_id=1, source_target_pairs={{0,2},{1,3},{2,0},{3,1},{4,6},{5,7},{6,4},{7,5},{8,10},{9,11},{10,... | collective-permute-start | bytes 393224 | tf_op jit(solution)/shard_map/ppermute | solution.py:21
  81.4 3.5 %collective-permute-done.20.refs_2_ = bf16[4,64,256]{2,1,0:T(8,128)(2,1)S(1)} collective-permute-done((bf16[4,64,256]{2,1,0:T(8,128)(2,1)S(1)}, bf16[4,64,256]{2,1,0:T(8,128)(2,1)S(1)}, u32[]{:S(2)}, u32[]{:S(2)}) %collective-permute-start.20) | collective-permute-done | bytes 131104 | tf_op jit(solution)/shard_map/ppermute | solution.py:21
  85.4 1.8 %collective-permute-done.47.refs_2_ = bf16[4,64,256]{2,1,0:T(8,128)(2,1)S(1)} collective-permute-done((bf16[4,64,256]{2,1,0:T(8,128)(2,1)S(1)}, bf16[4,64,256]{2,1,0:T(8,128)(2,1)S(1)}, u32[]{:S(2)}, u32[]{:S(2)}) %collective-permute-start.47) | collective-permute-done | bytes 131104 | tf_op jit(solution)/shard_map/ppermute | solution.py:21
  87.3 2.0 %shard_map.74 = (f32[4,64,256]{2,1,0:T(8,128)S(1)}, bf16[4,64,256]{2,1,0:T(8,128)(2,1)S(1)}, bf16[4,64,256]{2,1,0:T(8,128)(2,1)S(1)}) custom-call(s32[1]{0:T(128)} %bitcast.place_ref, s32[4]{0:T(128)S(1)} %copy-done.5, bf16[4,256,1024]{2,1,0:T(8,128)(2,1)S(1)} %copy-done.2, bf16[4,256,1024]{2,1,0:T(8,128)(2,1)S(1)} %copy-done.3, ...), custom_call_target="tpu_custom_call" | custom-call | flops 1073741824 | bytes 4718592 | tf_op jit(solution)/shard_map/pallas_call | solution.py:124
  89.7 3.5 %collective-permute-start.23 = (bf16[4,64,256]{2,1,0:T(8,128)(2,1)S(1)}, bf16[4,64,256]{2,1,0:T(8,128)(2,1)S(1)}, u32[]{:S(2)}, u32[]{:S(2)}) collective-permute-start(bf16[4,64,256]{2,1,0:T(8,128)(2,1)S(1)} %get-tuple-element.31), channel_id=1, source_target_pairs={{0,12},{4,0},{8,4},{12,8},{1,13},{5,1},{9,5},{13,9},{2,14},{6,2},{... | collective-permute-start | bytes 393224 | tf_op jit(solution)/shard_map/ppermute | solution.py:26
  93.2 2.0 %shard_map.81 = (f32[4,64,256]{2,1,0:T(8,128)S(1)}, bf16[4,64,256]{2,1,0:T(8,128)(2,1)S(1)}, bf16[4,64,256]{2,1,0:T(8,128)(2,1)S(1)}) custom-call(s32[1]{0:T(128)} %bitcast.place_ref, s32[4]{0:T(128)S(1)} %copy-done.5, bf16[4,256,1024]{2,1,0:T(8,128)(2,1)S(1)} %copy-done.2, bf16[4,256,1024]{2,1,0:T(8,128)(2,1)S(1)} %copy-done.3, ...), custom_call_target="tpu_custom_call" | custom-call | flops 1073741824 | bytes 4718592 | tf_op jit(solution)/shard_map/pallas_call | solution.py:124
  95.2 3.8 %collective-permute-start.50 = (bf16[4,64,256]{2,1,0:T(8,128)(2,1)S(1)}, bf16[4,64,256]{2,1,0:T(8,128)(2,1)S(1)}, u32[]{:S(2)}, u32[]{:S(2)}) collective-permute-start(bf16[4,64,256]{2,1,0:T(8,128)(2,1)S(1)} %get-tuple-element.41), channel_id=1, source_target_pairs={{0,12},{4,0},{8,4},{12,8},{1,13},{5,1},{9,5},{13,9},{2,14},{6,2},{... | collective-permute-start | bytes 393224 | tf_op jit(solution)/shard_map/ppermute | solution.py:26
  99.1 1.6 %collective-permute-start.25 = (bf16[4,64,256]{2,1,0:T(8,128)(2,1)S(1)}, bf16[4,64,256]{2,1,0:T(8,128)(2,1)S(1)}, u32[]{:S(2)}, u32[]{:S(2)}) collective-permute-start(bf16[4,64,256]{2,1,0:T(8,128)(2,1)S(1)} %fusion.2.refs_0_), channel_id=1, source_target_pairs={{0,2},{1,3},{2,0},{3,1},{4,6},{5,7},{6,4},{7,5},{8,10},{9,11},{10,... | collective-permute-start | bytes 393224 | tf_op jit(solution)/shard_map/ppermute | solution.py:21
  100.7 2.7 %collective-permute-done.49 = bf16[4,64,256]{2,1,0:T(8,128)(2,1)S(1)} collective-permute-done((bf16[4,64,256]{2,1,0:T(8,128)(2,1)S(1)}, bf16[4,64,256]{2,1,0:T(8,128)(2,1)S(1)}, u32[]{:S(2)}, u32[]{:S(2)}) %collective-permute-start.49) | collective-permute-done | bytes 131104 | tf_op jit(solution)/shard_map/ppermute | solution.py:26
  103.8 1.6 %collective-permute-start.52 = (bf16[4,64,256]{2,1,0:T(8,128)(2,1)S(1)}, bf16[4,64,256]{2,1,0:T(8,128)(2,1)S(1)}, u32[]{:S(2)}, u32[]{:S(2)}) collective-permute-start(bf16[4,64,256]{2,1,0:T(8,128)(2,1)S(1)} %fusion.5.refs_0_), channel_id=1, source_target_pairs={{0,2},{1,3},{2,0},{3,1},{4,6},{5,7},{6,4},{7,5},{8,10},{9,11},{10,... | collective-permute-start | bytes 393224 | tf_op jit(solution)/shard_map/ppermute | solution.py:21
  105.9 3.0 %collective-permute-done.52.refs_2_ = bf16[4,64,256]{2,1,0:T(8,128)(2,1)S(1)} collective-permute-done((bf16[4,64,256]{2,1,0:T(8,128)(2,1)S(1)}, bf16[4,64,256]{2,1,0:T(8,128)(2,1)S(1)}, u32[]{:S(2)}, u32[]{:S(2)}) %collective-permute-start.52) | collective-permute-done | bytes 131104 | tf_op jit(solution)/shard_map/ppermute | solution.py:21
  112.9 1.6 %collective-permute-start.55 = (f32[128,128]{1,0:T(8,128)S(1)}, f32[128,128]{1,0:T(8,128)S(1)}, u32[]{:S(2)}, u32[]{:S(2)}) collective-permute-start(f32[128,128]{1,0:T(8,128)S(1)} %add.60), channel_id=1, source_target_pairs={{0,2},{1,3},{2,0},{3,1},{4,6},{5,7},{6,4},{7,5},{8,10},{9,11},{10,... | collective-permute-start | bytes 196616 | tf_op jit(solution)/shard_map/ppermute | solution.py:21
  114.5 2.8 %collective-permute-done.55 = f32[128,128]{1,0:T(8,128)S(1)} collective-permute-done((f32[128,128]{1,0:T(8,128)S(1)}, f32[128,128]{1,0:T(8,128)S(1)}, u32[]{:S(2)}, u32[]{:S(2)}) %collective-permute-start.55) | collective-permute-done | bytes 65568 | tf_op jit(solution)/shard_map/ppermute | solution.py:21
  117.2 1.4 %collective-permute-start.56 = (f32[128,128]{1,0:T(8,128)S(1)}, f32[128,128]{1,0:T(8,128)S(1)}, u32[]{:S(2)}, u32[]{:S(2)}) collective-permute-start(f32[128,128]{1,0:T(8,128)S(1)} %add.61), channel_id=1, source_target_pairs={{0,4},{4,0},{8,12},{12,8},{1,5},{5,1},{9,13},{13,9},{2,6},{6,2},{1... | collective-permute-start | bytes 196616 | tf_op jit(solution)/shard_map/ppermute | solution.py:21
  118.7 2.9 %collective-permute-done.56 = f32[128,128]{1,0:T(8,128)S(1)} collective-permute-done((f32[128,128]{1,0:T(8,128)S(1)}, f32[128,128]{1,0:T(8,128)S(1)}, u32[]{:S(2)}, u32[]{:S(2)}) %collective-permute-start.56) | collective-permute-done | bytes 65568 | tf_op jit(solution)/shard_map/ppermute | solution.py:21
  121.6 2.5 %collective-permute-start.57 = (f32[128,128]{1,0:T(8,128)S(1)}, f32[128,128]{1,0:T(8,128)S(1)}, u32[]{:S(2)}, u32[]{:S(2)}) collective-permute-start(f32[128,128]{1,0:T(8,128)S(1)} %add.62), channel_id=1, source_target_pairs={{0,8},{4,12},{8,0},{12,4},{1,9},{5,13},{9,1},{13,5},{2,10},{6,14},... | collective-permute-start | bytes 196616 | tf_op jit(solution)/shard_map/ppermute | solution.py:21
  124.0 2.8 %collective-permute-done.57 = f32[128,128]{1,0:T(8,128)S(1)} collective-permute-done((f32[128,128]{1,0:T(8,128)S(1)}, f32[128,128]{1,0:T(8,128)S(1)}, u32[]{:S(2)}, u32[]{:S(2)}) %collective-permute-start.57) | collective-permute-done | bytes 65568 | tf_op jit(solution)/shard_map/ppermute | solution.py:21
  126.8 5.6 %shard_map.84 = (f32[4,256,128]{2,1,0:T(8,128)}, f32[128,128]{1,0:T(8,128)}) custom-call(f32[128,128]{1,0:T(8,128)S(1)} %add.63.gram_ref, f32[4,64,256]{2,1,0:T(8,128)S(1)} %shard_map.75.refs_0_, f32[4,64,256]{2,1,0:T(8,128)S(1)} %shard_map.82.refs_1_), custom_call_target="tpu_custom_call" | custom-call | tf_op jit(solution)/shard_map/pallas_call | solution.py:228
  (107 shorter events, 18.9 us)
Async XLA Ops:
  1.7 7.4 %collective-permute-start.1 = (bf16[4,64,256]{2,1,0:T(8,128)(2,1)S(1)}, bf16[4,64,256]{2,1,0:T(8,128)(2,1)S(1)}, u32[]{:S(2)}, u32[]{:S(2)}) collective-permute-start(bf16[4,64,256]{2,1,0:T(8,128)(2,1)S(1)} %get-tuple-element.22.refs_0_), channel_id=1, source_target_pairs={{0,2},{1,3},{2,0},{3,1},{4,6},{5,7},{6,4},{7,5},{8,10},{9,11},{10,... | collective-permute-start | bytes 393224 | tf_op jit(solution)/shard_map/ppermute | solution.py:21
  4.7 6.3 %collective-permute-start.28 = (bf16[4,64,256]{2,1,0:T(8,128)(2,1)S(1)}, bf16[4,64,256]{2,1,0:T(8,128)(2,1)S(1)}, u32[]{:S(2)}, u32[]{:S(2)}) collective-permute-start(bf16[4,64,256]{2,1,0:T(8,128)(2,1)S(1)} %get-tuple-element.32.refs_0_), channel_id=1, source_target_pairs={{0,2},{1,3},{2,0},{3,1},{4,6},{5,7},{6,4},{7,5},{8,10},{9,11},{10,... | collective-permute-start | bytes 393224 | tf_op jit(solution)/shard_map/ppermute | solution.py:21
  4.8 6.2 %collective-permute-start = (bf16[4,64,256]{2,1,0:T(8,128)(2,1)S(1)}, bf16[4,64,256]{2,1,0:T(8,128)(2,1)S(1)}, u32[]{:S(2)}, u32[]{:S(2)}) collective-permute-start(bf16[4,64,256]{2,1,0:T(8,128)(2,1)S(1)} %get-tuple-element.22.refs_0_), channel_id=1, source_target_pairs={{0,1},{1,0},{2,3},{3,2},{4,5},{5,4},{6,7},{7,6},{8,9},{9,8},{10,11... | collective-permute-start | bytes 393224 | tf_op jit(solution)/shard_map/ppermute | solution.py:21
  9.1 6.1 %collective-permute-start.27 = (bf16[4,64,256]{2,1,0:T(8,128)(2,1)S(1)}, bf16[4,64,256]{2,1,0:T(8,128)(2,1)S(1)}, u32[]{:S(2)}, u32[]{:S(2)}) collective-permute-start(bf16[4,64,256]{2,1,0:T(8,128)(2,1)S(1)} %get-tuple-element.32.refs_0_), channel_id=1, source_target_pairs={{0,1},{1,0},{2,3},{3,2},{4,5},{5,4},{6,7},{7,6},{8,9},{9,8},{10,11... | collective-permute-start | bytes 393224 | tf_op jit(solution)/shard_map/ppermute | solution.py:21
  11.0 4.2 %collective-permute-start.29 = (bf16[4,64,256]{2,1,0:T(8,128)(2,1)S(1)}, bf16[4,64,256]{2,1,0:T(8,128)(2,1)S(1)}, u32[]{:S(2)}, u32[]{:S(2)}) collective-permute-start(bf16[4,64,256]{2,1,0:T(8,128)(2,1)S(1)} %collective-permute-done.28.refs_2_), channel_id=1, source_target_pairs={{0,1},{1,0},{2,3},{3,2},{4,5},{5,4},{6,7},{7,6},{8,9},{9,8},{10,11... | collective-permute-start | bytes 393224 | tf_op jit(solution)/shard_map/ppermute | solution.py:21
  13.4 6.4 %collective-permute-start.4 = (bf16[4,64,256]{2,1,0:T(8,128)(2,1)S(1)}, bf16[4,64,256]{2,1,0:T(8,128)(2,1)S(1)}, u32[]{:S(2)}, u32[]{:S(2)}) collective-permute-start(bf16[4,64,256]{2,1,0:T(8,128)(2,1)S(1)} %shard_map.69.refs_0_), channel_id=1, source_target_pairs={{0,2},{1,3},{2,0},{3,1},{4,6},{5,7},{6,4},{7,5},{8,10},{9,11},{10,... | collective-permute-start | bytes 393224 | tf_op jit(solution)/shard_map/ppermute | solution.py:21
  16.0 6.2 %collective-permute-start.31 = (bf16[4,64,256]{2,1,0:T(8,128)(2,1)S(1)}, bf16[4,64,256]{2,1,0:T(8,128)(2,1)S(1)}, u32[]{:S(2)}, u32[]{:S(2)}) collective-permute-start(bf16[4,64,256]{2,1,0:T(8,128)(2,1)S(1)} %shard_map.76.refs_0_), channel_id=1, source_target_pairs={{0,2},{1,3},{2,0},{3,1},{4,6},{5,7},{6,4},{7,5},{8,10},{9,11},{10,... | collective-permute-start | bytes 393224 | tf_op jit(solution)/shard_map/ppermute | solution.py:21
  16.4 5.9 %collective-permute-start.3 = (bf16[4,64,256]{2,1,0:T(8,128)(2,1)S(1)}, bf16[4,64,256]{2,1,0:T(8,128)(2,1)S(1)}, u32[]{:S(2)}, u32[]{:S(2)}) collective-permute-start(bf16[4,64,256]{2,1,0:T(8,128)(2,1)S(1)} %shard_map.69.refs_0_), channel_id=1, source_target_pairs={{0,1},{1,0},{2,3},{3,2},{4,5},{5,4},{6,7},{7,6},{8,9},{9,8},{10,11... | collective-permute-start | bytes 393224 | tf_op jit(solution)/shard_map/ppermute | solution.py:21
  19.9 8.4 %collective-permute-start.30 = (bf16[4,64,256]{2,1,0:T(8,128)(2,1)S(1)}, bf16[4,64,256]{2,1,0:T(8,128)(2,1)S(1)}, u32[]{:S(2)}, u32[]{:S(2)}) collective-permute-start(bf16[4,64,256]{2,1,0:T(8,128)(2,1)S(1)} %shard_map.76.refs_0_), channel_id=1, source_target_pairs={{0,1},{1,0},{2,3},{3,2},{4,5},{5,4},{6,7},{7,6},{8,9},{9,8},{10,11... | collective-permute-start | bytes 393224 | tf_op jit(solution)/shard_map/ppermute | solution.py:21
  22.2 6.0 %collective-permute-start.32 = (bf16[4,64,256]{2,1,0:T(8,128)(2,1)S(1)}, bf16[4,64,256]{2,1,0:T(8,128)(2,1)S(1)}, u32[]{:S(2)}, u32[]{:S(2)}) collective-permute-start(bf16[4,64,256]{2,1,0:T(8,128)(2,1)S(1)} %collective-permute-done.31.refs_2_), channel_id=1, source_target_pairs={{0,1},{1,0},{2,3},{3,2},{4,5},{5,4},{6,7},{7,6},{8,9},{9,8},{10,11... | collective-permute-start | bytes 393224 | tf_op jit(solution)/shard_map/ppermute | solution.py:21
  24.3 9.9 %collective-permute-start.6 = (bf16[4,64,256]{2,1,0:T(8,128)(2,1)S(1)}, bf16[4,64,256]{2,1,0:T(8,128)(2,1)S(1)}, u32[]{:S(2)}, u32[]{:S(2)}) collective-permute-start(bf16[4,64,256]{2,1,0:T(8,128)(2,1)S(1)} %get-tuple-element.24), channel_id=1, source_target_pairs={{0,4},{4,8},{8,12},{12,0},{1,5},{5,9},{9,13},{13,1},{2,6},{6,10},{... | collective-permute-start | bytes 393224 | tf_op jit(solution)/shard_map/ppermute | solution.py:26
  26.1 9.3 %collective-permute-start.7 = (bf16[4,64,256]{2,1,0:T(8,128)(2,1)S(1)}, bf16[4,64,256]{2,1,0:T(8,128)(2,1)S(1)}, u32[]{:S(2)}, u32[]{:S(2)}) collective-permute-start(bf16[4,64,256]{2,1,0:T(8,128)(2,1)S(1)} %get-tuple-element.25), channel_id=1, source_target_pairs={{0,12},{4,0},{8,4},{12,8},{1,13},{5,1},{9,5},{13,9},{2,14},{6,2},{... | collective-permute-start | bytes 393224 | tf_op jit(solution)/shard_map/ppermute | solution.py:26
  30.2 8.3 %collective-permute-start.33 = (bf16[4,64,256]{2,1,0:T(8,128)(2,1)S(1)}, bf16[4,64,256]{2,1,0:T(8,128)(2,1)S(1)}, u32[]{:S(2)}, u32[]{:S(2)}) collective-permute-start(bf16[4,64,256]{2,1,0:T(8,128)(2,1)S(1)} %get-tuple-element.34), channel_id=1, source_target_pairs={{0,4},{4,8},{8,12},{12,0},{1,5},{5,9},{9,13},{13,1},{2,6},{6,10},{... | collective-permute-start | bytes 393224 | tf_op jit(solution)/shard_map/ppermute | solution.py:26
  30.3 9.9 %collective-permute-start.34 = (bf16[4,64,256]{2,1,0:T(8,128)(2,1)S(1)}, bf16[4,64,256]{2,1,0:T(8,128)(2,1)S(1)}, u32[]{:S(2)}, u32[]{:S(2)}) collective-permute-start(bf16[4,64,256]{2,1,0:T(8,128)(2,1)S(1)} %get-tuple-element.35), channel_id=1, source_target_pairs={{0,12},{4,0},{8,4},{12,8},{1,13},{5,1},{9,5},{13,9},{2,14},{6,2},{... | collective-permute-start | bytes 393224 | tf_op jit(solution)/shard_map/ppermute | solution.py:26
  35.5 6.3 %collective-permute-start.9 = (bf16[4,64,256]{2,1,0:T(8,128)(2,1)S(1)}, bf16[4,64,256]{2,1,0:T(8,128)(2,1)S(1)}, u32[]{:S(2)}, u32[]{:S(2)}) collective-permute-start(bf16[4,64,256]{2,1,0:T(8,128)(2,1)S(1)} %fusion.refs_0_), channel_id=1, source_target_pairs={{0,2},{1,3},{2,0},{3,1},{4,6},{5,7},{6,4},{7,5},{8,10},{9,11},{10,... | collective-permute-start | bytes 393224 | tf_op jit(solution)/shard_map/ppermute | solution.py:21
  40.3 5.0 %collective-permute-start.36 = (bf16[4,64,256]{2,1,0:T(8,128)(2,1)S(1)}, bf16[4,64,256]{2,1,0:T(8,128)(2,1)S(1)}, u32[]{:S(2)}, u32[]{:S(2)}) collective-permute-start(bf16[4,64,256]{2,1,0:T(8,128)(2,1)S(1)} %fusion.3.refs_0_), channel_id=1, source_target_pairs={{0,2},{1,3},{2,0},{3,1},{4,6},{5,7},{6,4},{7,5},{8,10},{9,11},{10,... | collective-permute-start | bytes 393224 | tf_op jit(solution)/shard_map/ppermute | solution.py:21
  42.3 5.3 %collective-permute-start.35 = (bf16[4,64,256]{2,1,0:T(8,128)(2,1)S(1)}, bf16[4,64,256]{2,1,0:T(8,128)(2,1)S(1)}, u32[]{:S(2)}, u32[]{:S(2)}) collective-permute-start(bf16[4,64,256]{2,1,0:T(8,128)(2,1)S(1)} %fusion.3.refs_0_), channel_id=1, source_target_pairs={{0,1},{1,0},{2,3},{3,2},{4,5},{5,4},{6,7},{7,6},{8,9},{9,8},{10,11... | collective-permute-start | bytes 393224 | tf_op jit(solution)/shard_map/ppermute | solution.py:21
  46.1 6.4 %collective-permute-start.12 = (bf16[4,64,256]{2,1,0:T(8,128)(2,1)S(1)}, bf16[4,64,256]{2,1,0:T(8,128)(2,1)S(1)}, u32[]{:S(2)}, u32[]{:S(2)}) collective-permute-start(bf16[4,64,256]{2,1,0:T(8,128)(2,1)S(1)} %shard_map.71.refs_0_), channel_id=1, source_target_pairs={{0,2},{1,3},{2,0},{3,1},{4,6},{5,7},{6,4},{7,5},{8,10},{9,11},{10,... | collective-permute-start | bytes 393224 | tf_op jit(solution)/shard_map/ppermute | solution.py:21
  48.4 6.4 %collective-permute-start.39 = (bf16[4,64,256]{2,1,0:T(8,128)(2,1)S(1)}, bf16[4,64,256]{2,1,0:T(8,128)(2,1)S(1)}, u32[]{:S(2)}, u32[]{:S(2)}) collective-permute-start(bf16[4,64,256]{2,1,0:T(8,128)(2,1)S(1)} %shard_map.78.refs_0_), channel_id=1, source_target_pairs={{0,2},{1,3},{2,0},{3,1},{4,6},{5,7},{6,4},{7,5},{8,10},{9,11},{10,... | collective-permute-start | bytes 393224 | tf_op jit(solution)/shard_map/ppermute | solution.py:21
  49.0 5.9 %collective-permute-start.11 = (bf16[4,64,256]{2,1,0:T(8,128)(2,1)S(1)}, bf16[4,64,256]{2,1,0:T(8,128)(2,1)S(1)}, u32[]{:S(2)}, u32[]{:S(2)}) collective-permute-start(bf16[4,64,256]{2,1,0:T(8,128)(2,1)S(1)} %shard_map.71.refs_0_), channel_id=1, source_target_pairs={{0,1},{1,0},{2,3},{3,2},{4,5},{5,4},{6,7},{7,6},{8,9},{9,8},{10,11... | collective-permute-start | bytes 393224 | tf_op jit(solution)/shard_map/ppermute | solution.py:21
  52.5 8.2 %collective-permute-start.38 = (bf16[4,64,256]{2,1,0:T(8,128)(2,1)S(1)}, bf16[4,64,256]{2,1,0:T(8,128)(2,1)S(1)}, u32[]{:S(2)}, u32[]{:S(2)}) collective-permute-start(bf16[4,64,256]{2,1,0:T(8,128)(2,1)S(1)} %shard_map.78.refs_0_), channel_id=1, source_target_pairs={{0,1},{1,0},{2,3},{3,2},{4,5},{5,4},{6,7},{7,6},{8,9},{9,8},{10,11... | collective-permute-start | bytes 393224 | tf_op jit(solution)/shard_map/ppermute | solution.py:21
  54.9 5.9 %collective-permute-start.40 = (bf16[4,64,256]{2,1,0:T(8,128)(2,1)S(1)}, bf16[4,64,256]{2,1,0:T(8,128)(2,1)S(1)}, u32[]{:S(2)}, u32[]{:S(2)}) collective-permute-start(bf16[4,64,256]{2,1,0:T(8,128)(2,1)S(1)} %collective-permute-done.39.refs_2_), channel_id=1, source_target_pairs={{0,1},{1,0},{2,3},{3,2},{4,5},{5,4},{6,7},{7,6},{8,9},{9,8},{10,11... | collective-permute-start | bytes 393224 | tf_op jit(solution)/shard_map/ppermute | solution.py:21
  56.9 9.8 %collective-permute-start.14 = (bf16[4,64,256]{2,1,0:T(8,128)(2,1)S(1)}, bf16[4,64,256]{2,1,0:T(8,128)(2,1)S(1)}, u32[]{:S(2)}, u32[]{:S(2)}) collective-permute-start(bf16[4,64,256]{2,1,0:T(8,128)(2,1)S(1)} %get-tuple-element.27), channel_id=1, source_target_pairs={{0,4},{4,8},{8,12},{12,0},{1,5},{5,9},{9,13},{13,1},{2,6},{6,10},{... | collective-permute-start | bytes 393224 | tf_op jit(solution)/shard_map/ppermute | solution.py:26
  58.5 9.4 %collective-permute-start.15 = (bf16[4,64,256]{2,1,0:T(8,128)(2,1)S(1)}, bf16[4,64,256]{2,1,0:T(8,128)(2,1)S(1)}, u32[]{:S(2)}, u32[]{:S(2)}) collective-permute-start(bf16[4,64,256]{2,1,0:T(8,128)(2,1)S(1)} %get-tuple-element.28), channel_id=1, source_target_pairs={{0,12},{4,0},{8,4},{12,8},{1,13},{5,1},{9,5},{13,9},{2,14},{6,2},{... | collective-permute-start | bytes 393224 | tf_op jit(solution)/shard_map/ppermute | solution.py:26
  62.7 8.3 %collective-permute-start.41 = (bf16[4,64,256]{2,1,0:T(8,128)(2,1)S(1)}, bf16[4,64,256]{2,1,0:T(8,128)(2,1)S(1)}, u32[]{:S(2)}, u32[]{:S(2)}) collective-permute-start(bf16[4,64,256]{2,1,0:T(8,128)(2,1)S(1)} %get-tuple-element.37), channel_id=1, source_target_pairs={{0,4},{4,8},{8,12},{12,0},{1,5},{5,9},{9,13},{13,1},{2,6},{6,10},{... | collective-permute-start | bytes 393224 | tf_op jit(solution)/shard_map/ppermute | solution.py:26
  62.8 9.8 %collective-permute-start.42 = (bf16[4,64,256]{2,1,0:T(8,128)(2,1)S(1)}, bf16[4,64,256]{2,1,0:T(8,128)(2,1)S(1)}, u32[]{:S(2)}, u32[]{:S(2)}) collective-permute-start(bf16[4,64,256]{2,1,0:T(8,128)(2,1)S(1)} %get-tuple-element.38), channel_id=1, source_target_pairs={{0,12},{4,0},{8,4},{12,8},{1,13},{5,1},{9,5},{13,9},{2,14},{6,2},{... | collective-permute-start | bytes 393224 | tf_op jit(solution)/shard_map/ppermute | solution.py:26
  68.0 6.3 %collective-permute-start.17 = (bf16[4,64,256]{2,1,0:T(8,128)(2,1)S(1)}, bf16[4,64,256]{2,1,0:T(8,128)(2,1)S(1)}, u32[]{:S(2)}, u32[]{:S(2)}) collective-permute-start(bf16[4,64,256]{2,1,0:T(8,128)(2,1)S(1)} %fusion.1.refs_0_), channel_id=1, source_target_pairs={{0,2},{1,3},{2,0},{3,1},{4,6},{5,7},{6,4},{7,5},{8,10},{9,11},{10,... | collective-permute-start | bytes 393224 | tf_op jit(solution)/shard_map/ppermute | solution.py:21
  72.7 5.0 %collective-permute-start.44 = (bf16[4,64,256]{2,1,0:T(8,128)(2,1)S(1)}, bf16[4,64,256]{2,1,0:T(8,128)(2,1)S(1)}, u32[]{:S(2)}, u32[]{:S(2)}) collective-permute-start(bf16[4,64,256]{2,1,0:T(8,128)(2,1)S(1)} %fusion.4.refs_0_), channel_id=1, source_target_pairs={{0,2},{1,3},{2,0},{3,1},{4,6},{5,7},{6,4},{7,5},{8,10},{9,11},{10,... | collective-permute-start | bytes 393224 | tf_op jit(solution)/shard_map/ppermute | solution.py:21
  74.2 3.5 %collective-permute-start.16 = (bf16[4,64,256]{2,1,0:T(8,128)(2,1)S(1)}, bf16[4,64,256]{2,1,0:T(8,128)(2,1)S(1)}, u32[]{:S(2)}, u32[]{:S(2)}) collective-permute-start(bf16[4,64,256]{2,1,0:T(8,128)(2,1)S(1)} %fusion.1.refs_0_), channel_id=1, source_target_pairs={{0,1},{1,0},{2,3},{3,2},{4,5},{5,4},{6,7},{7,6},{8,9},{9,8},{10,11... | collective-permute-start | bytes 393224 | tf_op jit(solution)/shard_map/ppermute | solution.py:21
  74.2 3.5 %collective-permute-start.18 = (bf16[4,64,256]{2,1,0:T(8,128)(2,1)S(1)}, bf16[4,64,256]{2,1,0:T(8,128)(2,1)S(1)}, u32[]{:S(2)}, u32[]{:S(2)}) collective-permute-start(bf16[4,64,256]{2,1,0:T(8,128)(2,1)S(1)} %collective-permute-done.17.refs_2_), channel_id=1, source_target_pairs={{0,1},{1,0},{2,3},{3,2},{4,5},{5,4},{6,7},{7,6},{8,9},{9,8},{10,11... | collective-permute-start | bytes 393224 | tf_op jit(solution)/shard_map/ppermute | solution.py:21
  74.7 5.3 %collective-permute-start.43 = (bf16[4,64,256]{2,1,0:T(8,128)(2,1)S(1)}, bf16[4,64,256]{2,1,0:T(8,128)(2,1)S(1)}, u32[]{:S(2)}, u32[]{:S(2)}) collective-permute-start(bf16[4,64,256]{2,1,0:T(8,128)(2,1)S(1)} %fusion.4.refs_0_), channel_id=1, source_target_pairs={{0,1},{1,0},{2,3},{3,2},{4,5},{5,4},{6,7},{7,6},{8,9},{9,8},{10,11... | collective-permute-start | bytes 393224 | tf_op jit(solution)/shard_map/ppermute | solution.py:21
  78.5 6.4 %collective-permute-start.20 = (bf16[4,64,256]{2,1,0:T(8,128)(2,1)S(1)}, bf16[4,64,256]{2,1,0:T(8,128)(2,1)S(1)}, u32[]{:S(2)}, u32[]{:S(2)}) collective-permute-start(bf16[4,64,256]{2,1,0:T(8,128)(2,1)S(1)} %shard_map.73.refs_0_), channel_id=1, source_target_pairs={{0,2},{1,3},{2,0},{3,1},{4,6},{5,7},{6,4},{7,5},{8,10},{9,11},{10,... | collective-permute-start | bytes 393224 | tf_op jit(solution)/shard_map/ppermute | solution.py:21
  80.8 6.4 %collective-permute-start.47 = (bf16[4,64,256]{2,1,0:T(8,128)(2,1)S(1)}, bf16[4,64,256]{2,1,0:T(8,128)(2,1)S(1)}, u32[]{:S(2)}, u32[]{:S(2)}) collective-permute-start(bf16[4,64,256]{2,1,0:T(8,128)(2,1)S(1)} %shard_map.80.refs_0_), channel_id=1, source_target_pairs={{0,2},{1,3},{2,0},{3,1},{4,6},{5,7},{6,4},{7,5},{8,10},{9,11},{10,... | collective-permute-start | bytes 393224 | tf_op jit(solution)/shard_map/ppermute | solution.py:21
  81.4 5.9 %collective-permute-start.19 = (bf16[4,64,256]{2,1,0:T(8,128)(2,1)S(1)}, bf16[4,64,256]{2,1,0:T(8,128)(2,1)S(1)}, u32[]{:S(2)}, u32[]{:S(2)}) collective-permute-start(bf16[4,64,256]{2,1,0:T(8,128)(2,1)S(1)} %shard_map.73.refs_0_), channel_id=1, source_target_pairs={{0,1},{1,0},{2,3},{3,2},{4,5},{5,4},{6,7},{7,6},{8,9},{9,8},{10,11... | collective-permute-start | bytes 393224 | tf_op jit(solution)/shard_map/ppermute | solution.py:21
  84.9 8.2 %collective-permute-start.46 = (bf16[4,64,256]{2,1,0:T(8,128)(2,1)S(1)}, bf16[4,64,256]{2,1,0:T(8,128)(2,1)S(1)}, u32[]{:S(2)}, u32[]{:S(2)}) collective-permute-start(bf16[4,64,256]{2,1,0:T(8,128)(2,1)S(1)} %shard_map.80.refs_0_), channel_id=1, source_target_pairs={{0,1},{1,0},{2,3},{3,2},{4,5},{5,4},{6,7},{7,6},{8,9},{9,8},{10,11... | collective-permute-start | bytes 393224 | tf_op jit(solution)/shard_map/ppermute | solution.py:21
  87.3 5.9 %collective-permute-start.48 = (bf16[4,64,256]{2,1,0:T(8,128)(2,1)S(1)}, bf16[4,64,256]{2,1,0:T(8,128)(2,1)S(1)}, u32[]{:S(2)}, u32[]{:S(2)}) collective-permute-start(bf16[4,64,256]{2,1,0:T(8,128)(2,1)S(1)} %collective-permute-done.47.refs_2_), channel_id=1, source_target_pairs={{0,1},{1,0},{2,3},{3,2},{4,5},{5,4},{6,7},{7,6},{8,9},{9,8},{10,11... | collective-permute-start | bytes 393224 | tf_op jit(solution)/shard_map/ppermute | solution.py:21
  89.3 9.8 %collective-permute-start.22 = (bf16[4,64,256]{2,1,0:T(8,128)(2,1)S(1)}, bf16[4,64,256]{2,1,0:T(8,128)(2,1)S(1)}, u32[]{:S(2)}, u32[]{:S(2)}) collective-permute-start(bf16[4,64,256]{2,1,0:T(8,128)(2,1)S(1)} %get-tuple-element.30), channel_id=1, source_target_pairs={{0,4},{4,8},{8,12},{12,0},{1,5},{5,9},{9,13},{13,1},{2,6},{6,10},{... | collective-permute-start | bytes 393224 | tf_op jit(solution)/shard_map/ppermute | solution.py:26
  89.7 9.4 %collective-permute-start.23 = (bf16[4,64,256]{2,1,0:T(8,128)(2,1)S(1)}, bf16[4,64,256]{2,1,0:T(8,128)(2,1)S(1)}, u32[]{:S(2)}, u32[]{:S(2)}) collective-permute-start(bf16[4,64,256]{2,1,0:T(8,128)(2,1)S(1)} %get-tuple-element.31), channel_id=1, source_target_pairs={{0,12},{4,0},{8,4},{12,8},{1,13},{5,1},{9,5},{13,9},{2,14},{6,2},{... | collective-permute-start | bytes 393224 | tf_op jit(solution)/shard_map/ppermute | solution.py:26
  95.1 8.3 %collective-permute-start.49 = (bf16[4,64,256]{2,1,0:T(8,128)(2,1)S(1)}, bf16[4,64,256]{2,1,0:T(8,128)(2,1)S(1)}, u32[]{:S(2)}, u32[]{:S(2)}) collective-permute-start(bf16[4,64,256]{2,1,0:T(8,128)(2,1)S(1)} %get-tuple-element.40), channel_id=1, source_target_pairs={{0,4},{4,8},{8,12},{12,0},{1,5},{5,9},{9,13},{13,1},{2,6},{6,10},{... | collective-permute-start | bytes 393224 | tf_op jit(solution)/shard_map/ppermute | solution.py:26
  95.2 8.5 %collective-permute-start.50 = (bf16[4,64,256]{2,1,0:T(8,128)(2,1)S(1)}, bf16[4,64,256]{2,1,0:T(8,128)(2,1)S(1)}, u32[]{:S(2)}, u32[]{:S(2)}) collective-permute-start(bf16[4,64,256]{2,1,0:T(8,128)(2,1)S(1)} %get-tuple-element.41), channel_id=1, source_target_pairs={{0,12},{4,0},{8,4},{12,8},{1,13},{5,1},{9,5},{13,9},{2,14},{6,2},{... | collective-permute-start | bytes 393224 | tf_op jit(solution)/shard_map/ppermute | solution.py:26
  99.1 6.3 %collective-permute-start.25 = (bf16[4,64,256]{2,1,0:T(8,128)(2,1)S(1)}, bf16[4,64,256]{2,1,0:T(8,128)(2,1)S(1)}, u32[]{:S(2)}, u32[]{:S(2)}) collective-permute-start(bf16[4,64,256]{2,1,0:T(8,128)(2,1)S(1)} %fusion.2.refs_0_), channel_id=1, source_target_pairs={{0,2},{1,3},{2,0},{3,1},{4,6},{5,7},{6,4},{7,5},{8,10},{9,11},{10,... | collective-permute-start | bytes 393224 | tf_op jit(solution)/shard_map/ppermute | solution.py:21
  103.8 5.0 %collective-permute-start.52 = (bf16[4,64,256]{2,1,0:T(8,128)(2,1)S(1)}, bf16[4,64,256]{2,1,0:T(8,128)(2,1)S(1)}, u32[]{:S(2)}, u32[]{:S(2)}) collective-permute-start(bf16[4,64,256]{2,1,0:T(8,128)(2,1)S(1)} %fusion.5.refs_0_), channel_id=1, source_target_pairs={{0,2},{1,3},{2,0},{3,1},{4,6},{5,7},{6,4},{7,5},{8,10},{9,11},{10,... | collective-permute-start | bytes 393224 | tf_op jit(solution)/shard_map/ppermute | solution.py:21
  105.4 3.5 %collective-permute-start.24 = (bf16[4,64,256]{2,1,0:T(8,128)(2,1)S(1)}, bf16[4,64,256]{2,1,0:T(8,128)(2,1)S(1)}, u32[]{:S(2)}, u32[]{:S(2)}) collective-permute-start(bf16[4,64,256]{2,1,0:T(8,128)(2,1)S(1)} %fusion.2.refs_0_), channel_id=1, source_target_pairs={{0,1},{1,0},{2,3},{3,2},{4,5},{5,4},{6,7},{7,6},{8,9},{9,8},{10,11... | collective-permute-start | bytes 393224 | tf_op jit(solution)/shard_map/ppermute | solution.py:21
  105.4 3.5 %collective-permute-start.26 = (bf16[4,64,256]{2,1,0:T(8,128)(2,1)S(1)}, bf16[4,64,256]{2,1,0:T(8,128)(2,1)S(1)}, u32[]{:S(2)}, u32[]{:S(2)}) collective-permute-start(bf16[4,64,256]{2,1,0:T(8,128)(2,1)S(1)} %collective-permute-done.25.refs_2_), channel_id=1, source_target_pairs={{0,1},{1,0},{2,3},{3,2},{4,5},{5,4},{6,7},{7,6},{8,9},{9,8},{10,11... | collective-permute-start | bytes 393224 | tf_op jit(solution)/shard_map/ppermute | solution.py:21
  105.9 3.8 %collective-permute-start.51 = (bf16[4,64,256]{2,1,0:T(8,128)(2,1)S(1)}, bf16[4,64,256]{2,1,0:T(8,128)(2,1)S(1)}, u32[]{:S(2)}, u32[]{:S(2)}) collective-permute-start(bf16[4,64,256]{2,1,0:T(8,128)(2,1)S(1)} %fusion.5.refs_0_), channel_id=1, source_target_pairs={{0,1},{1,0},{2,3},{3,2},{4,5},{5,4},{6,7},{7,6},{8,9},{9,8},{10,11... | collective-permute-start | bytes 393224 | tf_op jit(solution)/shard_map/ppermute | solution.py:21
  112.9 4.3 %collective-permute-start.55 = (f32[128,128]{1,0:T(8,128)S(1)}, f32[128,128]{1,0:T(8,128)S(1)}, u32[]{:S(2)}, u32[]{:S(2)}) collective-permute-start(f32[128,128]{1,0:T(8,128)S(1)} %add.60), channel_id=1, source_target_pairs={{0,2},{1,3},{2,0},{3,1},{4,6},{5,7},{6,4},{7,5},{8,10},{9,11},{10,... | collective-permute-start | bytes 196616 | tf_op jit(solution)/shard_map/ppermute | solution.py:21
  117.2 4.3 %collective-permute-start.56 = (f32[128,128]{1,0:T(8,128)S(1)}, f32[128,128]{1,0:T(8,128)S(1)}, u32[]{:S(2)}, u32[]{:S(2)}) collective-permute-start(f32[128,128]{1,0:T(8,128)S(1)} %add.61), channel_id=1, source_target_pairs={{0,4},{4,0},{8,12},{12,8},{1,5},{5,1},{9,13},{13,9},{2,6},{6,2},{1... | collective-permute-start | bytes 196616 | tf_op jit(solution)/shard_map/ppermute | solution.py:21
  121.6 5.2 %collective-permute-start.57 = (f32[128,128]{1,0:T(8,128)S(1)}, f32[128,128]{1,0:T(8,128)S(1)}, u32[]{:S(2)}, u32[]{:S(2)}) collective-permute-start(f32[128,128]{1,0:T(8,128)S(1)} %add.62), channel_id=1, source_target_pairs={{0,8},{4,12},{8,0},{12,4},{1,9},{5,13},{9,1},{13,5},{2,10},{6,14},... | collective-permute-start | bytes 196616 | tf_op jit(solution)/shard_map/ppermute | solution.py:21
  (16 other events, 73.8 us)
